TPU v7x, 32 devices: a whole 2x2x4 slice. The times are simulated.
32 devices in a mesh: dom: 32 (over z, y, x, core).
Axes of the slice: x: 2, y: 2, z: 4, core: 2. Of those that a mesh axis runs over, the one named last changes fastest.
Arguments:
- rest_pos: float32 [3, 131072], P(None, 'dom'), may hold values from -6 to 6
- displacement: float32 [3, 131072], P(None, 'dom'), may hold values from -3 to 3
- velocity: float32 [3, 131072], P(None, 'dom'), may hold values from -6 to 6
- ext_force: float32 [3, 131072], P(None, 'dom'), may hold values from -6 to 6
- node_mass: float32 [131072], P('dom'), may hold values from 0.5 to 2
- body_accel: float32 [3], replicated, may hold values from -2 to 2
- connectivity: int32 [8, 131072], P(None, 'dom'), may hold values from 0 to 4095
- elem_material: int32 [1024], P('dom'), may hold values from 0 to 7
- stiffness: float32 [8, 24, 24], replicated, may hold values from -1.25 to 1.25
- shared_nodes: int32 [32, 5, 128], P('dom'), may hold values from 0 to 4095, as said below
- contact_slave: int32 [65536], P('dom'), may hold values from 0 to 4095
- contact_owner: int32 [65536, 1], P('dom'), may hold values from 0 to 31; in each aligned block of 2048 rows (0 to 2047, 2048 to 4095, ...) at most 256 rows name the same one
- contact_master: int32 [65536], P('dom'), may hold values from 0 to 4095
- contact_normal: float32 [3, 65536], P(None, 'dom'), may hold values from -4 to 4
- part_of_node: int32 [131072], P('dom'), may hold values from 0 to 799
- part_mass: float32 [400], replicated, may hold values from 81 to 327
- part_center: float32 [3, 400], replicated, may hold values from -1 to 1
- part_inertia: float32 [3, 400], replicated, may hold values from 81 to 327
Outputs:
- nodal_velocity: float32 [3, 131072], P(None, 'dom')
- part_motion: float32 [6, 400], replicated
Inputs may be any that keep to these rules, and one draw needn't show every extreme that they name: `connectivity`: offsets are taken modulo 4096 after adding the element's own local number. `shared_nodes`: on each partition d the 5 x 128 entries are distinct interface copies; entry k of list b on d and entry k of list b on d XOR 2**b are copies of one node. `contact_slave`: slave indices are local copies of the contact's own partition. `contact_owner`: among the 2048 contacts of one partition no owner appears more than 256 times, and some owner appears exactly 256 times. `contact_master`: master indices are local copies of the owner partition. `part_of_node`: values of 400 or more mark copies of no rigid part.
All inputs are finite; a program needn't handle non-finite values.
Results may differ from a plain program's by a relative error of at most 0.0001.
Values sent between devices are 32-bit elements; how exact they have to be, the bound alone decides.
A program may use at most 128 MiB of HBM per device.

v0:
```python
import functools

import jax
import jax.numpy as jnp
from jax import lax
from jax.experimental import pallas as pl
from jax.experimental.pallas import tpu as pltpu
from jax.sharding import PartitionSpec as P

CYCLES = 3
PARTS_SIZE = 400
TIME_STEP = 0.1
DAMP_RATIO = 0.05
PENALTY = 2.0
GAP_WIDTH = 0.5
CONTACT_DAMP = 0.2
L = 128
GROUP = 4
F32 = jnp.float32
BF16 = jnp.bfloat16
NT = (((1,), (1,)), ((), ()))


def lookup(tables, index):
    high = index >> 7
    low = index & 127
    found = [None] * len(tables[0])
    for r, rows in enumerate(tables):
        hit = high == r
        for c, row in enumerate(rows):
            got = jnp.take_along_axis(
                jnp.broadcast_to(row, index.shape), low, axis=1, mode="promise_in_bounds"
            )
            found[c] = got if found[c] is None else jnp.where(hit, got, found[c])
    return found


def table_rows(refs, rows):
    return [[ref(r) for ref in refs] for r in range(rows)]


def scatter_tile(index, values, rows, pieces, live=None):
    high = (index >> 7).astype(F32)
    low = (index & 127).astype(F32)
    sublane = lax.broadcasted_iota(jnp.int32, (max(rows, 16), L), 0).astype(F32).astype(BF16)
    place = lax.broadcasted_iota(jnp.int32, (L, L), 0).astype(F32).astype(BF16)
    one, zero = jnp.ones((), BF16), jnp.zeros((), BF16)
    parts = []
    for value in values:
        value = jnp.concatenate(value, 0) if isinstance(value, list) else value
        for p in range(pieces):
            piece = value.astype(BF16).astype(F32) if p + 1 < pieces else value
            parts.append(piece)
            value = value - piece
    left, right = [], []

    def spread(value, s, count):
        row = jnp.broadcast_to(value[s : s + 1, :], (16, L)).astype(BF16)
        return jnp.concatenate([row] * (count // 16), 0) if count > 16 else row

    for s in range(live or index.shape[0]):
        mine = sublane == spread(high, s, sublane.shape[0])
        left.append(jnp.concatenate(
            [jnp.where(mine, spread(part, s, sublane.shape[0]), zero) for part in parts], 0))
        right.append(jnp.where(place == spread(low, s, L), one, zero))
    return lax.dot_general(
        jnp.concatenate(left, 1), jnp.concatenate(right, 1), NT, preferred_element_type=F32
    )


def unstack(total, count, rows, pieces):
    out = []
    step = max(rows, 16)
    for c in range(count):
        base = c * pieces * step
        value = total[base : base + rows]
        for p in range(1, pieces):
            value = value + total[base + p * step : base + p * step + rows]
        out.append(value)
    return out


def advance(u, v, internal, received, shared, ext, mass, accel, rows, neighbours):
    added = unstack(scatter_tile(shared, received, rows, 3, neighbours), 3, rows, 3)
    assembled = [internal[c] + added[c] for c in range(3)]
    v = [v[c] + TIME_STEP * ((ext[c] - assembled[c]) / mass - accel[c]) for c in range(3)]
    u = [u[c] + TIME_STEP * v[c] for c in range(3)]
    return u, v, assembled


def by_part(rec_ref):
    return [[rec_ref[b, c : c + 1, :] for b in range(rec_ref.shape[0])] for c in range(3)]


def elem_body(first, neighbours, *refs):
    if first:
        u_ref, v_ref, corner_ref, shared_ref, matrix_ref, out_ref, own_ref, field, total = refs
        u = [u_ref[c] for c in range(3)]
        v = [v_ref[c] for c in range(3)]
    else:
        (u_ref, v_ref, corner_ref, shared_ref, matrix_ref, int_ref, rec_ref, ext_ref, mass_ref,
         accel_ref, out_ref, own_ref, un_ref, vn_ref, field, total) = refs
        rows = u_ref.shape[1]
        u, v, _ = advance(
            [u_ref[c] for c in range(3)], [v_ref[c] for c in range(3)],
            [int_ref[c] for c in range(3)], by_part(rec_ref), shared_ref[...],
            [ext_ref[c] for c in range(3)], mass_ref[...], [accel_ref[c] for c in range(3)],
            rows, neighbours)
        for c in range(3):
            un_ref[c] = u[c]
            vn_ref[c] = v[c]
    rows = u_ref.shape[1]
    for c in range(3):
        field[c] = u[c] + DAMP_RATIO * v[c]
    total[...] = jnp.zeros_like(total)
    blocks = corner_ref.shape[1] // L

    def corner_index(b):
        return corner_ref[:, pl.ds(pl.multiple_of(b * L, L), L)]

    def forces(b):
        found = lookup(
            table_rows([lambda r, c=c: field[c, r : r + 1, :] for c in range(3)], rows),
            corner_index(b))
        g = jnp.concatenate(found, 0)
        g_hi = g.astype(BF16).astype(F32)
        rhs = jnp.concatenate([g_hi, g - g_hi, g_hi, jnp.zeros((8, L), F32)], 0).astype(BF16)
        h = jnp.dot(matrix_ref[b], rhs, preferred_element_type=F32)
        return h[0:8], h[8:16], h[16:24]

    def group(i):
        each = [forces(i * GROUP + k) for k in range(GROUP)]
        return tuple(jnp.concatenate([h[c] for h in each], 0) for c in range(3))

    def add_group(i, held):
        index = jnp.concatenate([corner_index(i * GROUP + k) for k in range(GROUP)], 0)
        total[...] += scatter_tile(index, list(held), rows, 2)

    def step(i, held):
        coming = group(i)
        add_group(i - 1, held)
        return coming

    groups = blocks // GROUP
    add_group(groups - 1, lax.fori_loop(1, groups, step, group(0)))
    internal = unstack(total[...], 3, rows, 2)
    for c in range(3):
        out_ref[c] = internal[c]
        field[c] = internal[c]
    own = lookup(
        table_rows([lambda r, c=c: field[c, r : r + 1, :] for c in range(3)], rows),
        shared_ref[...])
    for b in range(neighbours):
        for c in range(3):
            own_ref[b, c : c + 1, :] = own[c][b : b + 1, :]


def slots_body(owner_ref, master_ref, normal_ref, slot_ref, pay_ref, *, domains, cap):
    tiles = owner_ref.shape[0]
    slot_rows = pay_ref.shape[1]
    domain = lax.broadcasted_iota(jnp.int32, (domains, L), 0)
    tri = (lax.broadcasted_iota(jnp.int32, (L, L), 0) <= lax.broadcasted_iota(
        jnp.int32, (L, L), 1)).astype(F32).astype(BF16)
    seen = jnp.zeros((domains, 1), F32)
    for t in range(tiles):
        owner = owner_ref[t : t + 1, :]
        hit = domain == jnp.broadcast_to(owner, (domains, L))
        hits = jnp.where(hit, 1.0, 0.0)
        upto = jnp.dot(hits.astype(BF16), tri, preferred_element_type=F32) + seen
        rank = jnp.sum(jnp.where(hit, upto, 0.0), axis=0, keepdims=True) - 1.0
        slot_ref[t : t + 1, :] = owner * cap + rank.astype(jnp.int32)
        seen = seen + jnp.sum(hits, axis=1, keepdims=True)
    acc = None
    for t in range(0, tiles, 8):
        sl = slice(t, t + 8)
        values = [normal_ref[c, sl, :] for c in range(3)] + [master_ref[sl, :].astype(F32) + 1.0]
        got = scatter_tile(slot_ref[sl, :], values, slot_rows, 3)
        acc = got if acc is None else acc + got
    for c, value in enumerate(unstack(acc, 4, slot_rows, 3)):
        pay_ref[c] = value


def project_body(neighbours, u_ref, v_ref, shared_ref, int_ref, rec_ref, ext_ref, mass_ref,
                 accel_ref, rest_ref, slave_ref, slot_ref, normal_ref, x_ref, vn_ref, as_ref,
                 pay_ref):
    rows = u_ref.shape[1]
    slot_rows = pay_ref.shape[1]
    u, v, assembled = advance(
        [u_ref[c] for c in range(3)], [v_ref[c] for c in range(3)],
        [int_ref[c] for c in range(3)], by_part(rec_ref), shared_ref[...],
        [ext_ref[c] for c in range(3)], mass_ref[...], [accel_ref[c] for c in range(3)],
        rows, neighbours)
    for c in range(3):
        x_ref[c] = rest_ref[c] + u[c]
        vn_ref[c] = v[c]
        as_ref[c] = assembled[c]
    acc = None
    for t in range(0, slave_ref.shape[0], 8):
        sl = slice(t, t + 8)
        found = lookup(state_rows(x_ref, vn_ref, rows), slave_ref[sl, :])
        normal = [normal_ref[c, sl, :] for c in range(3)]
        along = sum(found[c] * normal[c] for c in range(3))
        speed = sum(found[3 + c] * normal[c] for c in range(3))
        got = scatter_tile(slot_ref[sl, :], [along, speed], slot_rows, 3)
        acc = got if acc is None else acc + got
    for c, value in enumerate(unstack(acc, 2, slot_rows, 3)):
        pay_ref[c] = value


def state_rows(x_ref, v_ref, rows):
    return table_rows(
        [lambda r, c=c: x_ref[c, r : r + 1, :] for c in range(3)]
        + [lambda r, c=c: v_ref[c, r : r + 1, :] for c in range(3)], rows)


def push_body(x_ref, v_ref, sent_ref, push_ref, force_ref, total):
    rows = x_ref.shape[1]
    total[...] = jnp.zeros_like(total)

    def step(i, carry):
        sl = pl.ds(pl.multiple_of(i * 8, 8), 8)
        coded = sent_ref[3, sl, :]
        master = jnp.maximum(coded - 0.5, 0.0).astype(jnp.int32)
        normal = [sent_ref[c, sl, :] for c in range(3)]
        found = lookup(state_rows(x_ref, v_ref, rows), master)
        gap = sent_ref[4, sl, :] - sum(found[c] * normal[c] for c in range(3))
        closing = sent_ref[5, sl, :] - sum(found[3 + c] * normal[c] for c in range(3))
        z = -gap / GAP_WIDTH
        soft = jnp.maximum(z, 0.0) + jnp.log1p(jnp.exp(-jnp.abs(z)))
        push = PENALTY * GAP_WIDTH * soft - CONTACT_DAMP * closing
        push = jnp.where(coded > 0.5, push, 0.0)
        push_ref[sl, :] = push
        total[...] += scatter_tile(master, [-push * normal[c] for c in range(3)], rows, 2)
        return carry

    lax.fori_loop(0, push_ref.shape[0] // 8, step, 0, unroll=4)
    for c, value in enumerate(unstack(total[...], 3, rows, 2)):
        force_ref[c] = value


def finish_body(x_ref, v_ref, as_ref, ext_ref, mass_ref, accel_ref, force_ref, push_ref, slot_ref,
                slave_ref, normal_ref, part_ref, nv_ref, sums_ref, vals, total):
    rows = x_ref.shape[1]
    push_rows = [[push_ref[r : r + 1, :]] for r in range(push_ref.shape[0])]
    acc = None
    for t in range(0, slave_ref.shape[0], 8):
        sl = slice(t, t + 8)
        push = lookup(push_rows, slot_ref[sl, :])[0]
        got = scatter_tile(slave_ref[sl, :], [push * normal_ref[c, sl, :] for c in range(3)],
                           rows, 2)
        acc = got if acc is None else acc + got
    slave_force = unstack(acc, 3, rows, 2)
    mass = mass_ref[...]
    x = [x_ref[c] for c in range(3)]
    net = []
    for c in range(3):
        force = force_ref[c] + slave_force[c]
        nv_ref[c] = v_ref[c] + TIME_STEP * force / mass
        net.append(ext_ref[c] - as_ref[c] + force - mass * accel_ref[c])
    turned = [x[1] * net[2] - x[2] * net[1], x[2] * net[0] - x[0] * net[2],
              x[0] * net[1] - x[1] * net[0]]
    for i, value in enumerate([mass] + [mass * x[c] for c in range(3)] + net + turned):
        vals[i] = value
    part_rows = sums_ref.shape[1]
    total[...] = jnp.zeros_like(total)

    def step(i, carry):
        sl = pl.ds(pl.multiple_of(i * 8, 8), 8)
        part = part_ref[sl, :]
        total[...] += scatter_tile(part, [vals[k, sl, :] for k in range(10)], part_rows, 3)
        return carry

    lax.fori_loop(0, rows // 8, step, 0, unroll=2)
    for k, value in enumerate(unstack(total[...], 10, part_rows, 3)):
        sums_ref[k] = value


def coords(index):
    return {"dom": index}


def greet(peers):
    barrier = pltpu.get_barrier_semaphore()
    for peer in peers:
        pl.semaphore_signal(barrier, inc=1, device_id=coords(peer),
                            device_id_type=pl.DeviceIdType.MESH)
    pl.semaphore_wait(barrier, len(peers))


def send(source, target, send_sem, recv_sem, peer):
    return pltpu.make_async_remote_copy(
        src_ref=source, dst_ref=target, send_sem=send_sem, recv_sem=recv_sem,
        device_id=coords(peer), device_id_type=pl.DeviceIdType.MESH)


def exchange_body(neighbours, own_ref, got_ref, send_sem, recv_sem):
    me = lax.axis_index("dom")
    peers = [me + (1 - 2 * ((me // 2**b) % 2)) * 2**b for b in range(neighbours)]
    greet(peers)
    copies = [send(own_ref.at[b], got_ref.at[b], send_sem.at[b], recv_sem.at[b], peers[b])
              for b in range(neighbours)]
    for copy in copies:
        copy.start()
    for copy in copies:
        copy.wait()


def swap_body(domains, in_ref, out_ref, send_sem, recv_sem, own_sem):
    me = lax.axis_index("dom")
    own = pltpu.make_async_copy(in_ref.at[me], out_ref.at[me], own_sem)
    own.start()
    peers = [(me + apart) % domains for apart in range(1, domains)]
    greet(peers)
    copies = [send(in_ref.at[peer], out_ref.at[me], send_sem.at[i], recv_sem.at[i], peer)
              for i, peer in enumerate(peers)]
    for copy in copies:
        copy.start()
    for copy in copies:
        copy.wait()
    own.wait()


def bit_groups(domains):
    bits = domains.bit_length() - 1
    groups, low = [], 0
    while low < bits:
        width = min(3, bits - low)
        if bits - low == 4:
            width = 2
        groups.append((low, width))
        low += width
    return groups


def total_body(domains, in_ref, out_ref, *scratch):
    groups = bit_groups(domains)
    held, partial, (send_sem, recv_sem, own_sem) = (
        scratch[:len(groups)], scratch[len(groups):2 * len(groups) - 1], scratch[-3:])
    me = lax.axis_index("dom")
    plans = []
    for low, width in groups:
        size = 2**width
        digit = (me // 2**low) % size
        base = me - digit * 2**low
        plans.append((digit, [base + ((digit + o) % size) * 2**low for o in range(1, size)]))
    greet([peer for _, peers in plans for peer in peers])
    source = in_ref
    place = 0
    for g, (digit, peers) in enumerate(plans):
        own = pltpu.make_async_copy(source, held[g].at[digit], own_sem.at[g])
        copies = [own]
        for i, peer in enumerate(peers):
            copies.append(send(source, held[g].at[digit], send_sem.at[place + i],
                               recv_sem.at[place + i], peer))
        place += len(peers)
        for copy in copies:
            copy.start()
        for copy in copies:
            copy.wait()
        value = held[g][0]
        for k in range(1, len(peers) + 1):
            value = value + held[g][k]
        if g + 1 < len(plans):
            partial[g][...] = value
            source = partial[g]
        else:
            out_ref[...] = value


VMEM = pl.BlockSpec(memory_space=pltpu.VMEM)
SMEM = pl.BlockSpec(memory_space=pltpu.SMEM)


def call(body, outs, scratch, specs, name, collective=None):
    return pl.pallas_call(
        body,
        out_shape=outs,
        in_specs=specs,
        out_specs=[VMEM] * len(outs),
        scratch_shapes=scratch,
        name=name,
        compiler_params=pltpu.CompilerParams(
            vmem_limit_bytes=48 * 2**20, collective_id=collective,
            has_side_effects=collective is not None),
    )


def cross_product(left, right):
    return jnp.stack([
        left[1] * right[2] - left[2] * right[1],
        left[2] * right[0] - left[0] * right[2],
        left[0] * right[1] - left[1] * right[0],
    ])


def f32(*shape):
    return jax.ShapeDtypeStruct(shape, F32)


def by_owner(payload, domains):
    count, slot_rows, _ = payload.shape
    each = slot_rows // domains
    return payload.reshape(count, domains, each, L).transpose(1, 0, 2, 3).reshape(
        domains, count * each, L)


def to_slots(payload, count):
    domains, each, _ = payload.shape
    each = each // count
    return payload.reshape(domains, count, each, L).transpose(1, 0, 2, 3).reshape(
        count, domains * each, L)


def swap(payload, domains, collective):
    return call(
        functools.partial(swap_body, domains), [f32(*payload.shape)],
        [pltpu.SemaphoreType.DMA((domains,))] * 2 + [pltpu.SemaphoreType.DMA], [VMEM], "swap",
        collective)(payload)[0]


def exchange(own):
    neighbours = own.shape[0]
    return call(
        functools.partial(exchange_body, neighbours), [f32(*own.shape)],
        [pltpu.SemaphoreType.DMA((neighbours,))] * 2, [VMEM], "exchange", 0)(own)[0]


def total_over(sums, domains):
    groups = bit_groups(domains)
    count = sum(2**width - 1 for _, width in groups)
    return call(
        functools.partial(total_body, domains), [f32(*sums.shape)],
        [pltpu.VMEM((2**width,) + sums.shape, F32) for _, width in groups]
        + [pltpu.VMEM(sums.shape, F32)] * (len(groups) - 1)
        + [pltpu.SemaphoreType.DMA((count,))] * 2 + [pltpu.SemaphoreType.DMA((len(groups),))],
        [VMEM], "total", 1)(sums)[0]


def per_device(rest_pos, displacement, velocity, ext_force, node_mass, body_accel, connectivity,
               elem_material, stiffness, shared_nodes, contact_slave, contact_owner,
               contact_master, contact_normal, part_of_node, part_mass, part_center,
               part_inertia):
    domains = lax.axis_size("dom")
    neighbours, shared_count = shared_nodes.shape[1:]
    nodes = displacement.shape[1]
    rows = nodes // L
    elems = connectivity.shape[1]
    blocks = elems // L
    contacts = contact_slave.shape[0]
    tiles = contacts // L
    cap = -(-(4 * contacts // domains) // L) * L
    slot_rows = domains * cap // L
    part_rows = -(-PARTS_SIZE // L)

    corners = (connectivity + jnp.arange(elems, dtype=jnp.int32)[None, :]) % nodes
    u = displacement.reshape(3, rows, L)
    v = velocity.reshape(3, rows, L)
    ext = ext_force.reshape(3, rows, L)
    rest = rest_pos.reshape(3, rows, L)
    mass = node_mass.reshape(rows, L)
    shared = jnp.concatenate(
        [shared_nodes[0], jnp.zeros((8 - neighbours, shared_count), jnp.int32)], 0)
    k_hi = lax.reduce_precision(stiffness, 8, 7)
    k_lo = stiffness - k_hi
    matrix = jnp.concatenate(
        [k_hi, k_hi, k_lo, jnp.zeros(stiffness.shape[:2] + (8,), F32)], 2).astype(BF16)
    materials = stiffness.shape[0]
    pick = (elem_material[:, None] == jnp.arange(materials, dtype=jnp.int32)[None]).astype(BF16)
    matrix = jnp.dot(pick, matrix.reshape(materials, -1), preferred_element_type=F32)
    matrix = matrix.astype(BF16).reshape(blocks, 24, 80)

    owner = contact_owner.reshape(tiles, L)
    master = contact_master.reshape(tiles, L)
    slave = contact_slave.reshape(tiles, L)
    normal = contact_normal.reshape(3, tiles, L)
    slot, early = call(
        functools.partial(slots_body, domains=domains, cap=cap),
        [jax.ShapeDtypeStruct((tiles, L), jnp.int32), f32(4, slot_rows, L)], [],
        [VMEM] * 3, "slots")(owner, master, normal)

    node_shape = f32(3, rows, L)
    own_shape = f32(neighbours, 8, L)
    scratch = [pltpu.VMEM((3, rows, L), F32), pltpu.VMEM((6 * rows, L), F32)]
    received = internal = None
    for cycle in range(CYCLES):
        if cycle == 0:
            internal, own = call(
                functools.partial(elem_body, True, neighbours), [node_shape, own_shape], scratch,
                [VMEM] * 5, "elements")(u, v, corners, shared, matrix)
        else:
            internal, own, u, v = call(
                functools.partial(elem_body, False, neighbours),
                [node_shape, own_shape, node_shape, node_shape], scratch,
                [VMEM] * 9 + [SMEM], "elements")(
                    u, v, corners, shared, matrix, internal, received, ext, mass, body_accel)
        received = exchange(own)

    x, v, assembled, late = call(
        functools.partial(project_body, neighbours),
        [node_shape, node_shape, node_shape, f32(2, slot_rows, L)], [],
        [VMEM] * 7 + [SMEM] + [VMEM] * 4, "project")(
            u, v, shared, internal, received, ext, mass, body_accel, rest, slave, slot, normal)
    sent = jnp.concatenate([early, late], 0)
    sent = to_slots(swap(by_owner(sent, domains), domains, 3), 6)
    push, force = call(
        push_body, [f32(slot_rows, L), node_shape], [pltpu.VMEM((6 * rows, L), F32)],
        [VMEM] * 3, "push")(x, v, sent)
    push = to_slots(swap(by_owner(push[None], domains), domains, 4), 1)[0]
    nodal_velocity, sums = call(
        finish_body, [node_shape, f32(10, part_rows, L)],
        [pltpu.VMEM((10, rows, L), F32), pltpu.VMEM((30 * max(part_rows, 16), L), F32)],
        [VMEM] * 5 + [SMEM] + [VMEM] * 6, "finish")(
            x, v, assembled, ext, mass, body_accel, force, push, slot, slave, normal,
            part_of_node.reshape(rows, L))
    totals = total_over(sums, domains).reshape(10, part_rows * L)[:, :PARTS_SIZE]
    mass_total = part_mass + totals[0]
    centre = (part_mass[None] * part_center + totals[1:4]) / mass_total[None]
    force_sum = totals[4:7]
    torque = totals[7:10] - cross_product(centre, force_sum)
    part_motion = jnp.concatenate([force_sum / mass_total[None], torque / part_inertia], 0)
    return nodal_velocity.reshape(3, nodes), part_motion


def solution(mesh):
    placed = (
        P(None, "dom"), P(None, "dom"), P(None, "dom"), P(None, "dom"), P("dom"), P(),
        P(None, "dom"), P("dom"), P(), P("dom", None, None), P("dom"), P("dom", None), P("dom"),
        P(None, "dom"), P("dom"), P(), P(), P(),
    )
    return jax.shard_map(
        per_device, mesh=mesh, in_specs=placed, out_specs=(P(None, "dom"), P()), check_vma=False
    )
```

profile of v0, /device:TPU:0, one launch (start us, length us, event | category | flops | bytes accessed | tf_op | source)
XLA Modules:
  0.0 96.3 jit_solution(3592226790236491351)
XLA Ops:
  0.6 0.9 reduce-precision_convert_fusion
  1.6 0.1 pad.11.clone
  1.6 0.1 maximum_maximum_fusion
  1.7 0.0 copy-start.16
  1.7 0.1 convert_element_type.9
  1.9 0.5 copy-done.16
  2.4 0.2 convolution_convert_fusion
  2.6 0.0 copy-start.15
  2.6 0.0 copy-start.6
  2.7 0.2 reshape.63.refs_4_
  2.9 0.4 copy-done.15
  3.3 0.2 copy-done.6
  3.6 0.1 add_select_fusion.refs_2_
  3.6 0.8 copy-done.7
  4.4 0.0 copy-done.8
  4.4 0.0 copy-start.10
  4.4 10.6 %elements.3 = (f32[3,32,128]{2,1,0:T(8,128)S(1)}, f32[5,8,128]{2,1,0:T(8,128)S(1)}) custom-call(f32[3,32,128]{2,1,0:T(8,128)S(1)} %get-tuple-element.50.refs_0_, f32[3,32,128]{2,1,0:T(8,128)S(1)} %get-tuple-element.49.refs_1_, s32[8,4096]{1,0:T(8,128)S(1)} %add_select_fusion.refs_2_, s32[8,128]{1,0:T(8,128)S(1)} %concatenate.13.refs_3_.shared_ref, ...), custom_call_target="tpu_custom_call" | custom-call | tf_op jit(solution)/shard_map/elements/pallas_call | solution.py:487
  15.1 7.4 %exchange.3.refs_6_ = f32[5,8,128]{2,1,0:T(8,128)S(1)} custom-call(f32[5,8,128]{2,1,0:T(8,128)S(1)} %get-tuple-element.23.own_ref), custom_call_target="tpu_custom_call" | custom-call | tf_op jit(solution)/shard_map/exchange/pallas_call | solution.py:423
  22.5 0.0 copy-start
  22.6 0.0 copy-start.3
  22.6 0.7 copy-done
  23.3 11.5 %elements.4 = (f32[3,32,128]{2,1,0:T(8,128)S(1)}, f32[5,8,128]{2,1,0:T(8,128)S(1)}, f32[3,32,128]{2,1,0:T(8,128)S(1)}, f32[3,32,128]{2,1,0:T(8,128)S(1)}) custom-call(f32[3,32,128]{2,1,0:T(8,128)S(1)} %get-tuple-element.50.refs_0_, f32[3,32,128]{2,1,0:T(8,128)S(1)} %get-tuple-element.49.refs_1_, s32[8,4096]{1,0:T(8,128)S(1)} %add_select_fusion.refs_2_, ...), custom_call_target="tpu_custom_call" | custom-call | tf_op jit(solution)/shard_map/elements/pallas_call | solution.py:491
  34.7 4.7 %exchange.4.refs_6_ = f32[5,8,128]{2,1,0:T(8,128)S(1)} custom-call(f32[5,8,128]{2,1,0:T(8,128)S(1)} %get-tuple-element.27.own_ref), custom_call_target="tpu_custom_call" | custom-call | tf_op jit(solution)/shard_map/exchange/pallas_call | solution.py:423
  39.5 11.5 %elements.5 = (f32[3,32,128]{2,1,0:T(8,128)S(1)}, f32[5,8,128]{2,1,0:T(8,128)S(1)}, f32[3,32,128]{2,1,0:T(8,128)S(1)}, f32[3,32,128]{2,1,0:T(8,128)S(1)}) custom-call(f32[3,32,128]{2,1,0:T(8,128)S(1)} %get-tuple-element.24.refs_0_, f32[3,32,128]{2,1,0:T(8,128)S(1)} %get-tuple-element.25.refs_1_, s32[8,4096]{1,0:T(8,128)S(1)} %add_select_fusion.refs_2_, ...), custom_call_target="tpu_custom_call" | custom-call | tf_op jit(solution)/shard_map/elements/pallas_call | solution.py:491
  50.9 4.7 %exchange.5.rec_ref = f32[5,8,128]{2,1,0:T(8,128)S(1)} custom-call(f32[5,8,128]{2,1,0:T(8,128)S(1)} %get-tuple-element.31.own_ref), custom_call_target="tpu_custom_call" | custom-call | tf_op jit(solution)/shard_map/exchange/pallas_call | solution.py:423
  55.7 0.0 copy-start.4
  55.7 0.0 copy-start.5
  55.7 0.7 copy-done.4
  56.4 0.0 copy-done.5
  56.4 1.2 %slots.1 = (s32[16,128]{1,0:T(8,128)S(1)}, f32[4,64,128]{2,1,0:T(8,128)S(1)}) custom-call(s32[16,128]{1,0:T(8,128)S(1)} %bitcast.57, s32[16,128]{1,0:T(8,128)S(1)} %bitcast.58, f32[3,16,128]{2,1,0:T(8,128)S(1)} %bitcast.44), custom_call_target="tpu_custom_call" | custom-call | tf_op jit(solution)/shard_map/slots/pallas_call | solution.py:476
  57.7 1.8 %project.1 = (f32[3,32,128]{2,1,0:T(8,128)S(1)}, f32[3,32,128]{2,1,0:T(8,128)S(1)}, f32[3,32,128]{2,1,0:T(8,128)S(1)}, f32[2,64,128]{2,1,0:T(8,128)S(1)}) custom-call(f32[3,32,128]{2,1,0:T(8,128)S(1)} %get-tuple-element.28.u_ref, f32[3,32,128]{2,1,0:T(8,128)S(1)} %get-tuple-element.29.v_ref, s32[8,128]{1,0:T(8,128)S(1)} %concatenate.13.refs_3_.shared_ref, ...), custom_call_target="tpu_custom_call" | custom-call | tf_op jit(solution)/shard_map/project/pallas_call | solution.py:498
  59.5 0.1 copy.23.in_ref
  59.7 8.5 %swap.2 = f32[32,12,128]{2,1,0:T(8,128)S(1)} custom-call(f32[32,12,128]{2,1,0:T(8,128)S(1)} %copy.23.in_ref), custom_call_target="tpu_custom_call" | custom-call | tf_op jit(solution)/shard_map/swap/pallas_call | solution.py:415
  68.1 0.1 copy.24
  68.2 0.2 copy.25
  68.4 2.6 %push.1 = (f32[64,128]{1,0:T(8,128)S(1)}, f32[3,32,128]{2,1,0:T(8,128)S(1)}) custom-call(f32[3,32,128]{2,1,0:T(8,128)S(1)} %get-tuple-element.33.x_ref, f32[3,32,128]{2,1,0:T(8,128)S(1)} %get-tuple-element.34.v_ref, f32[6,64,128]{2,1,0:T(8,128)S(1)} %bitcast.43), custom_call_target="tpu_custom_call" | custom-call | tf_op jit(solution)/shard_map/push/pallas_call | solution.py:505
  70.9 0.0 copy-start.2
  70.9 9.6 %swap.3 = f32[32,2,128]{2,1,0:T(2,128)S(1)} custom-call(f32[32,2,128]{2,1,0:T(2,128)S(1)} %bitcast.55), custom_call_target="tpu_custom_call" | custom-call | tf_op jit(solution)/shard_map/swap/pallas_call | solution.py:415
  80.6 2.4 %finish.1 = (f32[3,32,128]{2,1,0:T(8,128)S(1)}, f32[10,4,128]{2,1,0:T(4,128)S(1)}) custom-call(f32[3,32,128]{2,1,0:T(8,128)S(1)} %get-tuple-element.33.x_ref, f32[3,32,128]{2,1,0:T(8,128)S(1)} %get-tuple-element.34.v_ref, f32[3,32,128]{2,1,0:T(8,128)S(1)} %get-tuple-element.35.as_ref, f32[3,32,128]{2,1,0:T(8,128)S(1)} %get-tuple-element.52.refs_7_.ext_ref, ...), custom_call_target="tpu_custom_call" | custom-call | tf_op jit(solution)/shard_map/finish/pallas_call | solution.py:509
  83.0 10.5 %total.1 = f32[10,4,128]{2,1,0:T(4,128)S(1)} custom-call(f32[10,4,128]{2,1,0:T(4,128)S(1)} %get-tuple-element.41.in_ref), custom_call_target="tpu_custom_call" | custom-call | tf_op jit(solution)/shard_map/total/pallas_call | solution.py:431
  93.6 0.0 copy-start.12
  93.6 0.0 copy-start.13
  93.6 0.6 copy-done.12
  94.2 0.0 copy-done.13
  94.3 0.0 copy-start.14
  94.3 0.7 copy-done.14
  95.0 0.6 pad_maximum_fusion.1
  95.6 0.7 copy.41
  (26 shorter events, 0.1 us)
Async XLA Ops:
  1.7 0.7 copy-start.16
  2.6 0.7 copy-start.15
  2.6 0.9 copy-start.6
  3.5 0.8 copy-start.7
  3.6 0.9 copy-start.8
  4.4 18.1 %copy-start.9 = (f32[3,4096]{1,0:T(4,128)S(1)}, f32[3,4096]{1,0:T(4,128)}, u32[]{:S(2)}) copy-start(f32[3,4096]{1,0:T(4,128)} %param.18) | copy-start | bytes 147460
  4.4 18.1 %copy-start.10 = (f32[3,4096]{1,0:T(4,128)S(1)}, f32[3,4096]{1,0:T(4,128)}, u32[]{:S(2)}) copy-start(f32[3,4096]{1,0:T(4,128)} %param.21) | copy-start | bytes 147460
  22.5 0.7 copy-start
  22.6 0.7 copy-start.3
  50.9 4.8 %copy-start.11 = (f32[3,2048]{1,0:T(4,128)S(1)}, f32[3,2048]{1,0:T(4,128)}, u32[]{:S(2)}) copy-start(f32[3,2048]{1,0:T(4,128)} %param.31) | copy-start | bytes 73732
  55.7 0.7 copy-start.4
  55.7 0.7 copy-start.5
  56.4 1.2 %copy-start.1 = (s32[2048]{0:T(1024)S(1)}, s32[2048]{0:T(1024)}, u32[]{:S(2)}) copy-start(s32[2048]{0:T(1024)} %param.28) | copy-start | bytes 24580
  70.9 9.6 %copy-start.2 = (s32[4096]{0:T(1024)S(1)}, s32[4096]{0:T(1024)}, u32[]{:S(2)}) copy-start(s32[4096]{0:T(1024)} %param.32) | copy-start | bytes 49156
  93.6 0.7 copy-start.12
  93.6 0.7 copy-start.13
  94.3 0.7 copy-start.14
where the time goes:
time: 96.8 us; the launch traced here: 96.3 us
  Pallas kernels  87.1 us (90%)
  local copies, waits for them, and re-layouts  6.25 us (6%)
  other arithmetic  1.75 us (2%)
  between operations  1 us (1%)
    pallas_call x2, Pallas kernels, per_device(): call(functools.partial(elem_body, False, neighbours), [node_shape, own_sh...  22.9 us
    pallas_call x2, Pallas kernels, swap(): call(functools.partial(swap_body, domains), [f32(*payload.shape)], [pltpu...  18.1 us
    pallas_call x3, Pallas kernels, exchange(): call(functools.partial(exchange_body, neighbours), [f32(*own.shape)], [pl...  16.9 us
    pallas_call x1, Pallas kernels, per_device(): call(functools.partial(elem_body, True, neighbours), [node_shape, own_sha...  10.6 us
    pallas_call x1, Pallas kernels, total_over(): call(functools.partial(total_body, domains), [f32(*sums.shape)], [pltpu.V...  10.5 us
    unnamed x39, local copies, waits for them, and re-layouts  5.43 us
    pallas_call x1, Pallas kernels, per_device(): call(push_body, [f32(slot_rows, L), node_shape], [pltpu.VMEM((6 * rows, L...  2.55 us
    pallas_call x1, Pallas kernels, per_device(): call(finish_body, [node_shape, f32(10, part_rows, L)], [pltpu.VMEM((10, r...  2.44 us

commit v1 on v0

v1 whole, which is shorter than its diff:
```python
import functools

import jax
import jax.numpy as jnp
from jax import lax
from jax.experimental import pallas as pl
from jax.experimental.pallas import tpu as pltpu
from jax.sharding import PartitionSpec as P

CYCLES = 3
PARTS_SIZE = 400
TIME_STEP = 0.1
DAMP_RATIO = 0.05
PENALTY = 2.0
GAP_WIDTH = 0.5
CONTACT_DAMP = 0.2
L = 128
GROUP = 4
F32 = jnp.float32
BF16 = jnp.bfloat16
NT = (((1,), (1,)), ((), ()))


def lookup(tables, index):
    high = index >> 7
    low = index & 127
    found = [None] * len(tables[0])
    for r, rows in enumerate(tables):
        hit = high == r
        for c, row in enumerate(rows):
            got = jnp.take_along_axis(
                jnp.broadcast_to(row, index.shape), low, axis=1, mode="promise_in_bounds"
            )
            found[c] = got if found[c] is None else jnp.where(hit, got, found[c])
    return found


def table_rows(refs, rows):
    return [[ref(r) for ref in refs] for r in range(rows)]


def scatter_tile(index, values, rows, pieces, live=None):
    high = (index >> 7).astype(F32)
    low = (index & 127).astype(F32)
    sublane = lax.broadcasted_iota(jnp.int32, (max(rows, 16), L), 0).astype(F32).astype(BF16)
    place = lax.broadcasted_iota(jnp.int32, (L, L), 0).astype(F32).astype(BF16)
    one, zero = jnp.ones((), BF16), jnp.zeros((), BF16)
    parts = []
    for value in values:
        value = jnp.concatenate(value, 0) if isinstance(value, list) else value
        for p in range(pieces):
            piece = value.astype(BF16).astype(F32) if p + 1 < pieces else value
            parts.append(piece)
            value = value - piece
    left, right = [], []

    def spread(value, s, count):
        row = jnp.broadcast_to(value[s : s + 1, :], (16, L)).astype(BF16)
        return jnp.concatenate([row] * (count // 16), 0) if count > 16 else row

    for s in range(live or index.shape[0]):
        mine = sublane == spread(high, s, sublane.shape[0])
        left.append(jnp.concatenate(
            [jnp.where(mine, spread(part, s, sublane.shape[0]), zero) for part in parts], 0))
        right.append(jnp.where(place == spread(low, s, L), one, zero))
    return lax.dot_general(
        jnp.concatenate(left, 1), jnp.concatenate(right, 1), NT, preferred_element_type=F32
    )


def unstack(total, count, rows, pieces):
    out = []
    step = max(rows, 16)
    for c in range(count):
        base = c * pieces * step
        value = total[base : base + rows]
        for p in range(1, pieces):
            value = value + total[base + p * step : base + p * step + rows]
        out.append(value)
    return out


def advance(u, v, internal, received, shared, ext, mass, accel, rows, neighbours):
    added = unstack(scatter_tile(shared, received, rows, 2, neighbours), 3, rows, 2)
    assembled = [internal[c] + added[c] for c in range(3)]
    v = [v[c] + TIME_STEP * ((ext[c] - assembled[c]) / mass - accel[c]) for c in range(3)]
    u = [u[c] + TIME_STEP * v[c] for c in range(3)]
    return u, v, assembled


def by_part(rec_ref):
    return [[rec_ref[b, c : c + 1, :] for b in range(rec_ref.shape[0])] for c in range(3)]


def corner_rows(conn_ref, b, nodes):
    start = pl.multiple_of(b * L, L)
    local = lax.broadcasted_iota(jnp.int32, (conn_ref.shape[0], L), 1) + start
    return lax.rem(conn_ref[:, pl.ds(start, L)] + local, nodes)


def split_matrix(stiff_ref, matrix_ref):
    for m in range(stiff_ref.shape[0]):
        k = stiff_ref[m]
        k_hi = k.astype(BF16).astype(F32)
        matrix_ref[m] = jnp.concatenate(
            [k_hi, k_hi, k - k_hi, jnp.zeros((k.shape[0], 8), F32)], 1).astype(BF16)


def internal_forces(field, total, conn_ref, material_ref, matrix_ref):
    rows = field.shape[1]
    nodes = rows * L
    total[...] = jnp.zeros_like(total)
    blocks = conn_ref.shape[1] // L

    def forces(b):
        found = lookup(
            table_rows([lambda r, c=c: field[c, r : r + 1, :] for c in range(3)], rows),
            corner_rows(conn_ref, b, nodes))
        g = jnp.concatenate(found, 0)
        g_hi = g.astype(BF16).astype(F32)
        rhs = jnp.concatenate([g_hi, g - g_hi, g_hi, jnp.zeros((8, L), F32)], 0).astype(BF16)
        h = jnp.dot(matrix_ref[material_ref[b]], rhs, preferred_element_type=F32)
        return h[0:8], h[8:16], h[16:24]

    def group(i):
        each = [forces(i * GROUP + k) for k in range(GROUP)]
        return tuple(jnp.concatenate([h[c] for h in each], 0) for c in range(3))

    def add_group(i, held):
        index = jnp.concatenate(
            [corner_rows(conn_ref, i * GROUP + k, nodes) for k in range(GROUP)], 0)
        total[...] += scatter_tile(index, list(held), rows, 2)

    def step(i, held):
        coming = group(i)
        add_group(i - 1, held)
        return coming

    groups = blocks // GROUP
    add_group(groups - 1, lax.fori_loop(1, groups, step, group(0)))
    return unstack(total[...], 3, rows, 2)


def shared_index(shared_ref):
    neighbours = shared_ref.shape[1]
    return jnp.concatenate(
        [shared_ref[0], jnp.zeros((8 - neighbours, shared_ref.shape[2]), jnp.int32)], 0)


def coords(index):
    return {"dom": index}


def greet(peers):
    barrier = pltpu.get_barrier_semaphore()
    for peer in peers:
        pl.semaphore_signal(barrier, inc=1, device_id=coords(peer),
                            device_id_type=pl.DeviceIdType.MESH)


def greeted(peers):
    pl.semaphore_wait(pltpu.get_barrier_semaphore(), len(peers))


def send(source, target, send_sem, recv_sem, peer):
    return pltpu.make_async_remote_copy(
        src_ref=source, dst_ref=target, send_sem=send_sem, recv_sem=recv_sem,
        device_id=coords(peer), device_id_type=pl.DeviceIdType.MESH)


def flips(me, neighbours):
    return [me + (1 - 2 * ((me // 2**b) % 2)) * 2**b for b in range(neighbours)]


def own_copies(own, rec_ref, send_sem, recv_sem, peers):
    return [send(own.at[b], rec_ref.at[b], send_sem.at[b], recv_sem.at[b], peer)
            for b, peer in enumerate(peers)]


def assemble(internal, int_ref, field, own, shared, neighbours):
    rows = field.shape[1]
    for c in range(3):
        int_ref[c] = internal[c]
        field[c] = internal[c]
    found = lookup(
        table_rows([lambda r, c=c: field[c, r : r + 1, :] for c in range(3)], rows), shared)
    for b in range(neighbours):
        for c in range(3):
            own[b, c : c + 1, :] = found[c][b : b + 1, :]


def put_slots(ref, at, value, each):
    for d in range(ref.shape[0]):
        ref[d, at * each : (at + 1) * each, :] = value[d * each : (d + 1) * each]


def slot_tile(ref, at, tile, each):
    step = 8 // each
    return jnp.concatenate(
        [ref[tile * step + j, at * each : (at + 1) * each, :] for j in range(step)], 0)


def slots(owner_ref, master_ref, normal_ref, slot_ref, pay, each):
    domains = pay.shape[0]
    tiles = owner_ref.shape[0]
    cap = each * L
    slot_rows = domains * each
    domain = lax.broadcasted_iota(jnp.int32, (domains, L), 0)
    tri = (lax.broadcasted_iota(jnp.int32, (L, L), 0) <= lax.broadcasted_iota(
        jnp.int32, (L, L), 1)).astype(F32).astype(BF16)
    seen = jnp.zeros((domains, 1), F32)
    for t in range(tiles):
        owner = owner_ref[t : t + 1, :]
        hit = domain == jnp.broadcast_to(owner, (domains, L))
        hits = jnp.where(hit, 1.0, 0.0)
        upto = jnp.dot(hits.astype(BF16), tri, preferred_element_type=F32) + seen
        rank = jnp.sum(jnp.where(hit, upto, 0.0), axis=0, keepdims=True) - 1.0
        slot_ref[t : t + 1, :] = owner * cap + rank.astype(jnp.int32)
        seen = seen + jnp.sum(hits, axis=1, keepdims=True)
    acc = None
    for t in range(0, tiles, 8):
        sl = slice(t, t + 8)
        values = [normal_ref[c, sl, :] for c in range(3)] + [master_ref[sl, :].astype(F32) + 1.0]
        got = scatter_tile(slot_ref[sl, :], values, slot_rows, 2)
        acc = got if acc is None else acc + got
    for c, value in enumerate(unstack(acc, 4, slot_rows, 2)):
        put_slots(pay, c, value, each)


def first_body(each, u_ref, v_ref, conn_ref, shared_ref, material_ref, stiff_ref, owner_ref,
               master_ref, normal_ref, int_ref, rec_ref, matrix_ref, slot_ref, early_ref, field,
               total, own, pay, send_sem, recv_sem, pay_send, pay_recv, own_sem):
    neighbours = shared_ref.shape[1]
    domains = pay.shape[0]
    me = lax.axis_index("dom")
    peers = [lax.rem(me + apart, domains) for apart in range(1, domains)]
    greet(peers)
    slots(owner_ref, master_ref, normal_ref, slot_ref, pay, each)
    split_matrix(stiff_ref, matrix_ref)
    for c in range(3):
        field[c] = u_ref[c] + DAMP_RATIO * v_ref[c]
    greeted(peers)
    early = [pltpu.make_async_copy(pay.at[me], early_ref.at[me], own_sem)]
    early += [send(pay.at[peer], early_ref.at[me], pay_send.at[i], pay_recv.at[i], peer)
              for i, peer in enumerate(peers)]
    for copy in early:
        copy.start()
    internal = internal_forces(field, total, conn_ref, material_ref, matrix_ref)
    assemble(internal, int_ref, field, own, shared_index(shared_ref), neighbours)
    copies = own_copies(own, rec_ref, send_sem, recv_sem, flips(me, neighbours))
    for copy in copies:
        copy.start()
    for copy in copies + early:
        copy.wait()


def next_body(u_ref, v_ref, conn_ref, shared_ref, material_ref, matrix_ref, old_ref, got_ref,
              ext_ref, mass_ref, accel_ref, int_ref, rec_ref, un_ref, vn_ref, field, total, own,
              send_sem, recv_sem):
    neighbours = shared_ref.shape[1]
    rows = u_ref.shape[1]
    me = lax.axis_index("dom")
    peers = flips(me, neighbours)
    greet(peers)
    shared = shared_index(shared_ref)
    u, v, _ = advance(
        [u_ref[c] for c in range(3)], [v_ref[c] for c in range(3)],
        [old_ref[c] for c in range(3)], by_part(got_ref), shared,
        [ext_ref[c] for c in range(3)], mass_ref[...], [accel_ref[c] for c in range(3)],
        rows, neighbours)
    for c in range(3):
        un_ref[c] = u[c]
        vn_ref[c] = v[c]
        field[c] = u[c] + DAMP_RATIO * v[c]
    internal = internal_forces(field, total, conn_ref, material_ref, matrix_ref)
    assemble(internal, int_ref, field, own, shared, neighbours)
    greeted(peers)
    copies = own_copies(own, rec_ref, send_sem, recv_sem, peers)
    for copy in copies:
        copy.start()
    for copy in copies:
        copy.wait()


def state_rows(x_ref, v_ref, rows):
    return table_rows(
        [lambda r, c=c: x_ref[c, r : r + 1, :] for c in range(3)]
        + [lambda r, c=c: v_ref[c, r : r + 1, :] for c in range(3)], rows)


def pushed(gap, closing):
    z = -gap / GAP_WIDTH
    soft = jnp.maximum(z, 0.0) + jnp.log1p(jnp.exp(-jnp.abs(z)))
    return PENALTY * GAP_WIDTH * soft - CONTACT_DAMP * closing


def bit_groups(domains):
    bits = domains.bit_length() - 1
    groups, low = [], 0
    while low < bits:
        width = min(3, bits - low)
        if bits - low == 4:
            width = 2
        groups.append((low, width))
        low += width
    return groups


def last_body(each, u_ref, v_ref, shared_ref, old_ref, got_ref, ext_ref, mass_ref, accel_ref,
              rest_ref, slave_ref, slot_ref, normal_ref, early_ref, part_ref, pmass_ref,
              pcentre_ref, pinertia_ref, nv_ref, motion_ref, x_ref, vn_ref, pay, back, slave_side,
              master_side, table, vals, total, sums, first, arrived, *scratch):
    domains = pay.shape[0]
    groups = bit_groups(domains)
    held, (pay_send, pay_recv, own_sem, sum_send, sum_recv, sum_own) = (
        scratch[:len(groups) - 1], scratch[len(groups) - 1:])
    held = (first,) + tuple(held)
    rows = u_ref.shape[1]
    slot_rows = domains * each
    neighbours = shared_ref.shape[1]
    me = lax.axis_index("dom")
    peers = [lax.rem(me + apart, domains) for apart in range(1, domains)]
    greet(peers)
    u, v, assembled = advance(
        [u_ref[c] for c in range(3)], [v_ref[c] for c in range(3)],
        [old_ref[c] for c in range(3)], by_part(got_ref), shared_index(shared_ref),
        [ext_ref[c] for c in range(3)], mass_ref[...], [accel_ref[c] for c in range(3)],
        rows, neighbours)
    mass = mass_ref[...]
    for c in range(3):
        x_ref[c] = rest_ref[c] + u[c]
        vn_ref[c] = v[c]
        vals[4 + c] = ext_ref[c] - assembled[c] - mass * accel_ref[c]
    acc = None
    for t in range(0, slave_ref.shape[0], 8):
        sl = slice(t, t + 8)
        found = lookup(state_rows(x_ref, vn_ref, rows), slave_ref[sl, :])
        normal = [normal_ref[c, sl, :] for c in range(3)]
        along = sum(found[c] * normal[c] for c in range(3))
        speed = sum(found[3 + c] * normal[c] for c in range(3))
        slave_side[0, sl, :] = along
        slave_side[1, sl, :] = speed
        got = scatter_tile(slot_ref[sl, :], [along, speed], slot_rows, 2)
        acc = got if acc is None else acc + got
    for c, value in enumerate(unstack(acc, 2, slot_rows, 2)):
        put_slots(pay, c, value, each)
    for t in range(slot_rows // 8):
        sl = slice(t * 8, t * 8 + 8)
        coded = slot_tile(early_ref, 3, t, each)
        master = jnp.maximum(coded - 0.5, 0.0).astype(jnp.int32)
        normal = [slot_tile(early_ref, c, t, each) for c in range(3)]
        found = lookup(state_rows(x_ref, vn_ref, rows), master)
        along = sum(found[c] * normal[c] for c in range(3))
        speed = sum(found[3 + c] * normal[c] for c in range(3))
        master_side[0, sl, :] = along
        master_side[1, sl, :] = speed
        step = 8 // each
        for j in range(step):
            pay[t * step + j, 2 * each : 3 * each, :] = along[j * each : (j + 1) * each]
            pay[t * step + j, 3 * each : 4 * each, :] = speed[j * each : (j + 1) * each]
    greeted(peers)
    copies = [pltpu.make_async_copy(pay.at[me], back.at[me], own_sem)]
    copies += [send(pay.at[peer], back.at[me], pay_send.at[i], pay_recv.at[i], peer)
               for i, peer in enumerate(peers)]
    for copy in copies:
        copy.start()
    vals[0] = mass
    for c in range(3):
        vals[1 + c] = mass * x_ref[c]
    for copy in copies:
        copy.wait()
    total[...] = jnp.zeros_like(total)
    for t in range(slot_rows // 8):
        sl = slice(t * 8, t * 8 + 8)
        for c in range(2):
            table[c, sl, :] = slot_tile(back, 2 + c, t, each)
        coded = slot_tile(early_ref, 3, t, each)
        master = jnp.maximum(coded - 0.5, 0.0).astype(jnp.int32)
        normal = [slot_tile(early_ref, c, t, each) for c in range(3)]
        push = pushed(slot_tile(back, 0, t, each) - master_side[0, sl, :],
                      slot_tile(back, 1, t, each) - master_side[1, sl, :])
        push = jnp.where(coded > 0.5, push, 0.0)
        total[...] += scatter_tile(master, [-push * normal[c] for c in range(3)], rows, 2)
    acc = None
    for t in range(0, slave_ref.shape[0], 8):
        sl = slice(t, t + 8)
        found = lookup(
            table_rows([lambda r, c=c: table[c, r : r + 1, :] for c in range(2)], slot_rows),
            slot_ref[sl, :])
        push = pushed(slave_side[0, sl, :] - found[0], slave_side[1, sl, :] - found[1])
        got = scatter_tile(slave_ref[sl, :], [push * normal_ref[c, sl, :] for c in range(3)],
                           rows, 2)
        acc = got if acc is None else acc + got
    contact = unstack(total[...] + acc, 3, rows, 2)
    x = [x_ref[c] for c in range(3)]
    net = []
    for c in range(3):
        nv_ref[c] = vn_ref[c] + TIME_STEP * contact[c] / mass
        net.append(vals[4 + c] + contact[c])
        vals[4 + c] = net[c]
    vals[7] = x[1] * net[2] - x[2] * net[1]
    vals[8] = x[2] * net[0] - x[0] * net[2]
    vals[9] = x[0] * net[1] - x[1] * net[0]
    part_rows = sums.shape[1]
    acc = None
    for t in range(0, rows, 8):
        sl = slice(t, t + 8)
        got = scatter_tile(part_ref[sl, :], [vals[k, sl, :] for k in range(10)], part_rows, 2)
        acc = got if acc is None else acc + got
    for k, value in enumerate(unstack(acc, 10, part_rows, 2)):
        sums[k] = value
    place = 0
    for g, (low, width) in enumerate(groups):
        size = 2**width
        digit = (me // 2**low) % size
        base = me - digit * 2**low
        copies = [pltpu.make_async_copy(sums, held[g].at[digit], sum_own.at[g])]
        for o in range(1, size):
            peer = base + ((digit + o) % size) * 2**low
            copies.append(send(sums, held[g].at[digit], sum_send.at[place],
                               sum_recv.at[place], peer))
            place += 1
        for copy in copies:
            copy.start()
        for copy in copies:
            copy.wait()
        value = held[g][0]
        for k in range(1, size):
            value = value + held[g][k]
        sums[...] = value
    arrived[...] = sums[...]
    for r in range(part_rows):
        wide = min(L, PARTS_SIZE - r * L)
        at = slice(r * L, r * L + wide)
        got = [arrived[k, r : r + 1, 0:wide] for k in range(10)]
        own_mass = pmass_ref[0:1, at]
        mass_total = own_mass + got[0]
        centre = [(own_mass * pcentre_ref[c : c + 1, at] + got[1 + c]) / mass_total
                  for c in range(3)]
        force = got[4:7]
        swept = [centre[1] * force[2] - centre[2] * force[1],
                 centre[2] * force[0] - centre[0] * force[2],
                 centre[0] * force[1] - centre[1] * force[0]]
        for c in range(3):
            motion_ref[c : c + 1, at] = force[c] / mass_total
            motion_ref[3 + c : 4 + c, at] = (got[7 + c] - swept[c]) / pinertia_ref[c : c + 1, at]


VMEM = pl.BlockSpec(memory_space=pltpu.VMEM)
SMEM = pl.BlockSpec(memory_space=pltpu.SMEM)


def call(body, outs, scratch, specs, name, collective=None):
    return pl.pallas_call(
        body,
        out_shape=outs,
        in_specs=specs,
        out_specs=[VMEM] * len(outs),
        scratch_shapes=scratch,
        name=name,
        compiler_params=pltpu.CompilerParams(
            vmem_limit_bytes=48 * 2**20, collective_id=collective,
            has_side_effects=collective is not None),
    )


def f32(*shape):
    return jax.ShapeDtypeStruct(shape, F32)


def per_device(rest_pos, displacement, velocity, ext_force, node_mass, body_accel, connectivity,
               elem_material, stiffness, shared_nodes, contact_slave, contact_owner,
               contact_master, contact_normal, part_of_node, part_mass, part_center,
               part_inertia):
    domains = lax.axis_size("dom")
    neighbours = shared_nodes.shape[1]
    nodes = displacement.shape[1]
    rows = nodes // L
    contacts = contact_slave.shape[0]
    tiles = contacts // L
    each = -(-(4 * contacts // domains) // L)
    slot_rows = domains * each
    part_rows = -(-PARTS_SIZE // L)
    dma = pltpu.SemaphoreType.DMA

    u = displacement.reshape(3, rows, L)
    v = velocity.reshape(3, rows, L)
    ext = ext_force.reshape(3, rows, L)
    rest = rest_pos.reshape(3, rows, L)
    mass = node_mass.reshape(rows, L)
    owner = contact_owner.reshape(tiles, L)
    master = contact_master.reshape(tiles, L)
    slave = contact_slave.reshape(tiles, L)
    normal = contact_normal.reshape(3, tiles, L)

    node_shape = f32(3, rows, L)
    rec_shape = f32(neighbours, 8, L)
    work = [pltpu.VMEM((3, rows, L), F32), pltpu.VMEM((6 * rows, L), F32),
            pltpu.VMEM((neighbours, 8, L), F32)]
    near = [dma((neighbours,))] * 2
    far = [dma((domains - 1,))] * 2 + [dma]
    materials, side = stiffness.shape[:2]
    internal, received, matrix, slot, early = call(
        functools.partial(first_body, each),
        [node_shape, rec_shape, jax.ShapeDtypeStruct((materials, side, 80), BF16),
         jax.ShapeDtypeStruct((tiles, L), jnp.int32), f32(domains, 4 * each, L)],
        work + [pltpu.VMEM((domains, 4 * each, L), F32)] + near + far,
        [VMEM] * 4 + [SMEM] + [VMEM] * 4, "first", 0)(
            u, v, connectivity, shared_nodes, elem_material, stiffness, owner, master, normal)
    for cycle in range(1, CYCLES):
        internal, received, u, v = call(
            next_body, [node_shape, rec_shape, node_shape, node_shape], work + near,
            [VMEM] * 4 + [SMEM] + [VMEM] * 5 + [SMEM], "next", 1)(
                u, v, connectivity, shared_nodes, elem_material, matrix, internal, received, ext,
                mass, body_accel)
    groups = bit_groups(domains)
    count = sum(2**width - 1 for _, width in groups)
    sum_shape = (10, part_rows, L)
    nodal_velocity, part_motion = call(
        functools.partial(last_body, each), [node_shape, f32(6, PARTS_SIZE)],
        [pltpu.VMEM((3, rows, L), F32)] * 2
        + [pltpu.VMEM((domains, 4 * each, L), F32)] * 2
        + [pltpu.VMEM((2, tiles, L), F32), pltpu.VMEM((2, slot_rows, L), F32),
           pltpu.VMEM((2, slot_rows, L), F32), pltpu.VMEM((10, rows, L), F32),
           pltpu.VMEM((6 * rows, L), F32), pltpu.VMEM(sum_shape, F32),
           pltpu.VMEM((2**groups[0][1],) + sum_shape, F32), pltpu.VMEM(sum_shape, F32)]
        + [pltpu.VMEM((2**width,) + sum_shape, F32) for _, width in groups[1:]]
        + far + [dma((count,))] * 2 + [dma((len(groups),))],
        [VMEM] * 7 + [SMEM] + [VMEM] * 9, "last", 2)(
            u, v, shared_nodes, internal, received, ext, mass, body_accel, rest, slave, slot,
            normal, early, part_of_node.reshape(rows, L), part_mass.reshape(1, PARTS_SIZE),
            part_center, part_inertia)
    return nodal_velocity.reshape(3, nodes), part_motion


def solution(mesh):
    placed = (
        P(None, "dom"), P(None, "dom"), P(None, "dom"), P(None, "dom"), P("dom"), P(),
        P(None, "dom"), P("dom"), P(), P("dom", None, None), P("dom"), P("dom", None), P("dom"),
        P(None, "dom"), P("dom"), P(), P(), P(),
    )
    return jax.shard_map(
        per_device, mesh=mesh, in_specs=placed, out_specs=(P(None, "dom"), P()), check_vma=False
    )
```

time: 96.8 us -> 79.1 us (0.82)
  Pallas kernels: 87.1 us -> 72.1 us
  other arithmetic: 1.75 us -> 0 us
    pallas_call x13 -> x4, Pallas kernels: 87.1 us -> 72.1 us  [the longest x2 29.4 us: per_device(): call(next_body, [node_shape, rec_shape, node_shape, node_shape], work + n...]
    unnamed x39 -> x34, local copies, waits for them, and re-layouts: 5.43 us -> 4.97 us
where the time goes in v1:
time: 79.1 us; the launch traced here: 78.8 us
  Pallas kernels  72.1 us (91%)
  local copies, waits for them, and re-layouts  5.88 us (7%)
  between operations  0.84 us (1%)
    pallas_call x2, Pallas kernels, per_device(): call(next_body, [node_shape, rec_shape, node_shape, node_shape], work + n...  29.4 us
    pallas_call x1, Pallas kernels, per_device(): call(functools.partial(last_body, each), [node_shape, f32(6, PARTS_SIZE)]...  21.5 us
    pallas_call x1, Pallas kernels, per_device(): call(functools.partial(first_body, each), [node_shape, rec_shape, jax.Sha...  21.3 us
    unnamed x34, local copies, waits for them, and re-layouts  4.97 us

profile of v1, /device:TPU:0, one launch (start us, length us, event | category | flops | bytes accessed | tf_op | source)
XLA Modules:
  0.0 78.8 jit_solution(13730780930950669193)
XLA Ops:
  0.6 0.0 copy-start.12
  0.6 0.7 copy.21.shared_ref
  1.4 0.8 copy.37
  2.1 0.0 copy-done.12
  2.1 0.0 copy-start.13
  2.1 0.0 copy-start.14
  2.1 0.0 copy-start.7
  2.1 0.0 copy-start.8
  2.1 0.9 %copy_bitcast_fusion.1 = (f32[3,32,128]{2,1,0:T(8,128)S(1)}, f32[3,32,128]{2,1,0:T(8,128)S(1)}) fusion(f32[1,3,32,128]{3,1,2,0:T(4,128)S(1)} %bitcast.37, f32[1,3,32,128]{3,1,2,0:T(4,128)} %bitcast.38), kind=kLoop, calls=%fused_computation.1 | loop fusion | bytes 196608 | tf_op jit(solution)/shard_map/reshape | solution.py:489
  3.1 0.0 copy-start
  3.1 0.0 copy-done.13
  3.1 0.0 copy-done.14
  3.1 0.0 copy-start.2
  3.1 0.0 copy-start.9
  3.1 0.0 copy-done.7
  3.1 0.0 copy-done.8
  3.1 0.8 %copy-done = s32[8,4096]{1,0:T(8,128)S(1)} copy-done((s32[8,4096]{1,0:T(8,128)S(1)}, s32[8,4096]{1,0:T(8,128)}, u32[]{:S(2)}) %copy-start) | copy-done | bytes 131096
  4.0 0.1 copy-done.2
  4.0 0.0 copy-done.9
  4.0 0.0 copy-start.1
  4.0 21.3 %first.1 = (f32[3,32,128]{2,1,0:T(8,128)S(1)}, f32[5,8,128]{2,1,0:T(8,128)S(1)}, bf16[8,24,80]{2,1,0:T(8,128)(2,1)S(1)}, s32[16,128]{1,0:T(8,128)S(1)}, f32[32,8,128]{2,1,0:T(8,128)S(1)}) custom-call(f32[3,32,128]{2,1,0:T(8,128)S(1)} %get-tuple-element.33.u_ref, f32[3,32,128]{2,1,0:T(8,128)S(1)} %get-tuple-element.32.v_ref, s32[8,4096]{1,0:T(8,128)S(1)} %copy-done, ...), custom_call_target="tpu_custom_call" | custom-call | tf_op jit(solution)/shard_map/first/pallas_call | solution.py:503
  25.3 0.0 copy-start.10
  25.3 0.0 copy-done.1
  25.3 0.6 copy-done.10
  26.0 15.5 %next.2 = (f32[3,32,128]{2,1,0:T(8,128)S(1)}, f32[5,8,128]{2,1,0:T(8,128)S(1)}, f32[3,32,128]{2,1,0:T(8,128)S(1)}, f32[3,32,128]{2,1,0:T(8,128)S(1)}) custom-call(f32[3,32,128]{2,1,0:T(8,128)S(1)} %get-tuple-element.33.u_ref, f32[3,32,128]{2,1,0:T(8,128)S(1)} %get-tuple-element.32.v_ref, s32[8,4096]{1,0:T(8,128)S(1)} %copy-done, ...), custom_call_target="tpu_custom_call" | custom-call | tf_op jit(solution)/shard_map/next/pallas_call | solution.py:511
  41.5 0.0 copy-start.3
  41.5 0.0 copy-start.4
  41.5 0.0 copy-start.5
  41.5 0.0 copy-start.6
  41.5 13.8 %next.3 = (f32[3,32,128]{2,1,0:T(8,128)S(1)}, f32[5,8,128]{2,1,0:T(8,128)S(1)}, f32[3,32,128]{2,1,0:T(8,128)S(1)}, f32[3,32,128]{2,1,0:T(8,128)S(1)}) custom-call(f32[3,32,128]{2,1,0:T(8,128)S(1)} %get-tuple-element.20.u_ref, f32[3,32,128]{2,1,0:T(8,128)S(1)} %get-tuple-element.21.v_ref, s32[8,4096]{1,0:T(8,128)S(1)} %copy-done, ...), custom_call_target="tpu_custom_call" | custom-call | tf_op jit(solution)/shard_map/next/pallas_call | solution.py:511
  55.4 0.0 copy-start.11
  55.4 0.0 copy-done.3
  55.4 0.0 copy-done.4
  55.4 0.0 copy-done.5
  55.4 0.0 copy-done.6
  55.4 0.6 copy-done.11
  56.1 21.5 %last.1 = (f32[3,32,128]{2,1,0:T(8,128)S(1)}, f32[6,400]{1,0:T(8,128)S(1)}) custom-call(f32[3,32,128]{2,1,0:T(8,128)S(1)} %get-tuple-element.24.u_ref, f32[3,32,128]{2,1,0:T(8,128)S(1)} %get-tuple-element.25.v_ref, s32[1,5,128]{2,1,0:T(8,128)S(1)} %copy.21.shared_ref, f32[3,32,128]{2,1,0:T(8,128)S(1)} %get-tuple-element.26.old_ref, ...), custom_call_target="tpu_custom_call" | custom-call | tf_op jit(solution)/shard_map/last/pallas_call | solution.py:519
  77.5 0.7 copy.36
  78.2 0.6 copy.39
  (1 shorter events, 0.0 us)
Async XLA Ops:
  0.6 1.5 %copy-start.12 = (f32[3,4096]{1,0:T(4,128)S(1)}, f32[3,4096]{1,0:T(4,128)}, u32[]{:S(2)}) copy-start(f32[3,4096]{1,0:T(4,128)} %param.18) | copy-start | bytes 147460
  2.1 0.9 %copy-start.13 = (f32[3,4096]{1,0:T(4,128)S(1)}, f32[3,4096]{1,0:T(4,128)}, u32[]{:S(2)}) copy-start(f32[3,4096]{1,0:T(4,128)} %param.20) | copy-start | bytes 147460
  2.1 1.0 %copy-start.14 = (f32[3,4096]{1,0:T(4,128)S(1)}, f32[3,4096]{1,0:T(4,128)}, u32[]{:S(2)}) copy-start(f32[3,4096]{1,0:T(4,128)} %param.19) | copy-start | bytes 147460
  2.1 1.0 %copy-start.7 = (s32[2048,1]{0,1:T(1,128)S(1)}, s32[2048,1]{0,1:T(1,128)}, u32[]{:S(2)}) copy-start(s32[2048,1]{0,1:T(1,128)} %param.29) | copy-start | bytes 24580
  2.1 1.0 %copy-start.8 = (s32[2048]{0:T(1024)S(1)}, s32[2048]{0:T(1024)}, u32[]{:S(2)}) copy-start(s32[2048]{0:T(1024)} %param.30) | copy-start | bytes 24580
  3.1 0.9 %copy-start = (s32[8,4096]{1,0:T(8,128)S(1)}, s32[8,4096]{1,0:T(8,128)}, u32[]{:S(2)}) copy-start(s32[8,4096]{1,0:T(8,128)} %conn_ref.5) | copy-start | bytes 393220
  3.1 0.9 %copy-start.2 = (f32[8,24,24]{2,1,0:T(8,128)S(1)}, f32[8,24,24]{2,1,0:T(8,128)}, u32[]{:S(2)}) copy-start(f32[8,24,24]{2,1,0:T(8,128)} %stiff_ref.1) | copy-start | bytes 55300
  3.1 0.9 %copy-start.9 = (s32[32]{0:T(128)S(1)}, s32[32]{0:T(128)}, u32[]{:S(2)}) copy-start(s32[32]{0:T(128)} %material_ref.5) | copy-start | bytes 388
  4.0 21.3 %copy-start.1 = (f32[4096]{0:T(1024)S(1)}, f32[4096]{0:T(1024)}, u32[]{:S(2)}) copy-start(f32[4096]{0:T(1024)} %param.22) | copy-start | bytes 49156
  25.3 0.7 copy-start.10
  41.5 13.9 %copy-start.3 = (s32[4096]{0:T(1024)S(1)}, s32[4096]{0:T(1024)}, u32[]{:S(2)}) copy-start(s32[4096]{0:T(1024)} %param.32) | copy-start | bytes 49156
  41.5 13.9 %copy-start.4 = (s32[2048]{0:T(1024)S(1)}, s32[2048]{0:T(1024)}, u32[]{:S(2)}) copy-start(s32[2048]{0:T(1024)} %param.28) | copy-start | bytes 24580
  41.5 13.9 %copy-start.5 = (f32[3,400]{1,0:T(4,128)S(1)}, f32[3,400]{1,0:T(4,128)}, u32[]{:S(2)}) copy-start(f32[3,400]{1,0:T(4,128)} %pcentre_ref.1) | copy-start | bytes 14404
  41.5 13.9 %copy-start.6 = (f32[3,400]{1,0:T(4,128)S(1)}, f32[3,400]{1,0:T(4,128)}, u32[]{:S(2)}) copy-start(f32[3,400]{1,0:T(4,128)} %pinertia_ref.1) | copy-start | bytes 14404
  55.4 0.7 copy-start.11

commit v2 on v1

v2 whole, which is shorter than its diff:
```python
import functools

import jax
import jax.numpy as jnp
from jax import lax
from jax.experimental import pallas as pl
from jax.experimental.pallas import tpu as pltpu
from jax.sharding import PartitionSpec as P

CYCLES = 3
PARTS_SIZE = 400
TIME_STEP = 0.1
DAMP_RATIO = 0.05
PENALTY = 2.0
GAP_WIDTH = 0.5
CONTACT_DAMP = 0.2
L = 128
GROUP = 4
F32 = jnp.float32
BF16 = jnp.bfloat16
NT = (((1,), (1,)), ((), ()))


def lookup(tables, index):
    high = index >> 7
    low = index & 127
    found = [None] * len(tables[0])
    for r, rows in enumerate(tables):
        hit = high == r
        for c, row in enumerate(rows):
            got = jnp.take_along_axis(
                jnp.broadcast_to(row, index.shape), low, axis=1, mode="promise_in_bounds"
            )
            found[c] = got if found[c] is None else jnp.where(hit, got, found[c])
    return found


def table_rows(refs, rows):
    return [[ref(r) for ref in refs] for r in range(rows)]


def spread(ref, row, count, *lead):
    one = jnp.broadcast_to(ref[(*lead, pl.ds(row, 1), slice(None))], (16, L)).astype(BF16)
    return jnp.concatenate([one] * (count // 16), 0) if count > 16 else one


def counting(rows):
    return lax.broadcasted_iota(jnp.int32, (rows, L), 0).astype(F32).astype(BF16)


def onehot_dot(count, rows, high, low, parts):
    height = max(rows, 16)
    sublane, place = counting(height), counting(L)
    one, zero = jnp.ones((), BF16), jnp.zeros((), BF16)
    left, right = [], []
    for s in range(count):
        mine = sublane == high(s, height)
        left.append(jnp.concatenate([jnp.where(mine, part(s, height), zero) for part in parts], 0))
        right.append(jnp.where(place == low(s, L), one, zero))
    return lax.dot_general(
        jnp.concatenate(left, 1), jnp.concatenate(right, 1), NT, preferred_element_type=F32)


def scatter_tile(index, values, rows, planes, slot, live=8):
    planes[slot, 0] = (index >> 7).astype(F32)
    planes[slot, 1] = (index & 127).astype(F32)
    for k, value in enumerate(values):
        value = jnp.concatenate(value, 0) if isinstance(value, list) else value
        top = value.astype(BF16).astype(F32)
        planes[slot, 2 + 2 * k, 0 : value.shape[0]] = top
        planes[slot, 3 + 2 * k, 0 : value.shape[0]] = value - top

    def row(k):
        return lambda s, height: spread(planes, s, height, slot, k)

    return onehot_dot(live, rows, row(0), row(1), [row(2 + k) for k in range(2 * len(values))])


def unstack(total, count, rows, pieces):
    out = []
    step = max(rows, 16)
    for c in range(count):
        base = c * pieces * step
        value = total[base : base + rows]
        for p in range(1, pieces):
            value = value + total[base + p * step : base + p * step + rows]
        out.append(value)
    return out


def advance(u, v, internal, received, shared, ext, mass, accel, rows, neighbours, planes):
    got = scatter_tile(shared, received, rows, planes, 0, neighbours)
    added = unstack(got, 3, rows, 2)
    assembled = [internal[c] + added[c] for c in range(3)]
    v = [v[c] + TIME_STEP * ((ext[c] - assembled[c]) / mass - accel[c]) for c in range(3)]
    u = [u[c] + TIME_STEP * v[c] for c in range(3)]
    return u, v, assembled


def by_part(rec_ref):
    return [[rec_ref[b, c : c + 1, :] for b in range(rec_ref.shape[0])] for c in range(3)]


def field_lookup(field, index):
    rows = field.shape[1]
    return lookup(
        table_rows([lambda r, c=c: field[c, r : r + 1, :] for c in range(3)], rows), index)


def prepare_corners(conn_ref, corner, high_ref, low_ref, nodes):
    for b in range(conn_ref.shape[1] // L):
        at = slice(b * L, (b + 1) * L)
        index = conn_ref[:, at] + (lax.broadcasted_iota(jnp.int32, (8, L), 1) + b * L)
        index = lax.rem(index, nodes)
        corner[:, at] = index
        high_ref[b * 8 : (b + 1) * 8, :] = (index >> 7).astype(F32)
        low_ref[b * 8 : (b + 1) * 8, :] = (index & 127).astype(F32)


def split_matrix(stiff_ref, matrix_ref):
    for m in range(stiff_ref.shape[0]):
        k = stiff_ref[m]
        k_hi = k.astype(BF16).astype(F32)
        matrix_ref[m] = jnp.concatenate(
            [k_hi, k_hi, k - k_hi, jnp.zeros((k.shape[0], 8), F32)], 1).astype(BF16)


def internal_forces(field, total, corner, high_ref, low_ref, material_ref, matrix_ref, pieces):
    rows = field.shape[1]
    total[...] = jnp.zeros_like(total)
    groups = corner.shape[1] // L // GROUP

    def group(i, slot):
        for k in range(GROUP):
            b = i * GROUP + k
            g = jnp.concatenate(
                field_lookup(field, corner[:, pl.ds(pl.multiple_of(b * L, L), L)]), 0)
            g_hi = g.astype(BF16).astype(F32)
            rhs = jnp.concatenate(
                [g_hi, g - g_hi, g_hi, jnp.zeros((8, L), F32)], 0).astype(BF16)
            h = jnp.dot(matrix_ref[material_ref[b]], rhs, preferred_element_type=F32)
            h_hi = h.astype(BF16).astype(F32)
            pieces[slot, 0, k * 24 : (k + 1) * 24, :] = h_hi
            pieces[slot, 1, k * 24 : (k + 1) * 24, :] = h - h_hi

    def add_group(i, slot):
        base = i * GROUP * 8

        def part(c, p):
            return lambda s, height: spread(
                pieces, (s // 8) * 24 + c * 8 + s % 8, height, slot, p)

        total[...] += onehot_dot(
            GROUP * 8, rows, lambda s, height: spread(high_ref, base + s, height),
            lambda s, height: spread(low_ref, base + s, height),
            [part(c, p) for c in range(3) for p in range(2)])

    def step(i, carry):
        group(2 * i + 1, 1)
        add_group(2 * i, 0)
        group(2 * i + 2, 0)
        add_group(2 * i + 1, 1)
        return carry

    group(0, 0)
    lax.fori_loop(0, groups // 2 - 1, step, 0)
    group(groups - 1, 1)
    add_group(groups - 2, 0)
    add_group(groups - 1, 1)
    return unstack(total[...], 3, rows, 2)


def shared_index(shared_ref):
    neighbours = shared_ref.shape[1]
    return jnp.concatenate(
        [shared_ref[0], jnp.zeros((8 - neighbours, shared_ref.shape[2]), jnp.int32)], 0)


def coords(index):
    return {"dom": index}


def greet(peers):
    barrier = pltpu.get_barrier_semaphore()
    for peer in peers:
        pl.semaphore_signal(barrier, inc=1, device_id=coords(peer),
                            device_id_type=pl.DeviceIdType.MESH)


def greeted(peers):
    pl.semaphore_wait(pltpu.get_barrier_semaphore(), len(peers))


def send(source, target, send_sem, recv_sem, peer):
    return pltpu.make_async_remote_copy(
        src_ref=source, dst_ref=target, send_sem=send_sem, recv_sem=recv_sem,
        device_id=coords(peer), device_id_type=pl.DeviceIdType.MESH)


def flips(me, neighbours):
    return [me + (1 - 2 * ((me // 2**b) % 2)) * 2**b for b in range(neighbours)]


def own_copies(own, rec_ref, send_sem, recv_sem, peers):
    return [send(own.at[b], rec_ref.at[b], send_sem.at[b], recv_sem.at[b], peer)
            for b, peer in enumerate(peers)]


def put_slots(ref, at, value, each):
    for d in range(ref.shape[0]):
        ref[d, at * each : (at + 1) * each, :] = value[d * each : (d + 1) * each]


def slot_tile(ref, at, tile, each):
    step = 8 // each
    return jnp.concatenate(
        [ref[tile * step + j, at * each : (at + 1) * each, :] for j in range(step)], 0)


def slots(owner_ref, master_ref, normal_ref, slot_ref, pay, each, planes):
    domains = pay.shape[0]
    tiles = owner_ref.shape[0]
    cap = each * L
    slot_rows = domains * each
    domain = lax.broadcasted_iota(jnp.int32, (domains, L), 0)
    tri = (lax.broadcasted_iota(jnp.int32, (L, L), 0) <= lax.broadcasted_iota(
        jnp.int32, (L, L), 1)).astype(F32).astype(BF16)
    seen = jnp.zeros((domains, 1), F32)
    for t in range(tiles):
        owner = owner_ref[t : t + 1, :]
        hit = domain == jnp.broadcast_to(owner, (domains, L))
        hits = jnp.where(hit, 1.0, 0.0)
        upto = jnp.dot(hits.astype(BF16), tri, preferred_element_type=F32) + seen
        rank = jnp.sum(jnp.where(hit, upto, 0.0), axis=0, keepdims=True) - 1.0
        slot_ref[t : t + 1, :] = owner * cap + rank.astype(jnp.int32)
        seen = seen + jnp.sum(hits, axis=1, keepdims=True)
    acc = None
    for t in range(0, tiles, 8):
        sl = slice(t, t + 8)
        values = [normal_ref[c, sl, :] for c in range(3)] + [master_ref[sl, :].astype(F32) + 1.0]
        got = scatter_tile(slot_ref[sl, :], values, slot_rows, planes, t // 8 % 4)
        acc = got if acc is None else acc + got
    for c, value in enumerate(unstack(acc, 4, slot_rows, 2)):
        put_slots(pay, c, value, each)


def state_rows(x_ref, v_ref, rows):
    return table_rows(
        [lambda r, c=c: x_ref[c, r : r + 1, :] for c in range(3)]
        + [lambda r, c=c: v_ref[c, r : r + 1, :] for c in range(3)], rows)


def pushed(gap, closing):
    z = -gap / GAP_WIDTH
    soft = jnp.maximum(z, 0.0) + jnp.log1p(jnp.exp(-jnp.abs(z)))
    return PENALTY * GAP_WIDTH * soft - CONTACT_DAMP * closing


def bit_groups(domains):
    bits = domains.bit_length() - 1
    groups, low = [], 0
    while low < bits:
        width = min(3, bits - low)
        if bits - low == 4:
            width = 2
        groups.append((low, width))
        low += width
    return groups


def part_sums(part_ref, vals, which, sums, planes):
    part_rows = sums.shape[1]
    acc = None
    for t in range(0, part_ref.shape[0], 8):
        sl = slice(t, t + 8)
        got = scatter_tile(
            part_ref[sl, :], [vals[k, sl, :] for k in which], part_rows, planes, t // 8 % 4)
        acc = got if acc is None else acc + got
    for k, value in zip(which, unstack(acc, len(which), part_rows, 2)):
        sums[k] = value


def window_body(each, u_ref, v_ref, rest_ref, ext_ref, mass_ref, accel_ref, conn_ref,
                material_ref, stiff_ref, shared_ref, slave_ref, owner_ref, master_ref, normal_ref,
                part_ref, pmass_ref, pcentre_ref, pinertia_ref, nv_ref, motion_ref, field, total,
                corner, high_ref, low_ref, pieces, matrix_ref, planes, own, rec, x_ref, vn_ref,
                slot_ref, ready, early_ref, pay, back, slave_side, master_side, table, vals, sums,
                first, *scratch):
    domains = pay.shape[0]
    groups = bit_groups(domains)
    held = (first,) + tuple(scratch[:len(groups) - 1])
    (near_send, near_recv, early_send, early_recv, early_own, pay_send, pay_recv, own_sem,
     sum_send, sum_recv, sum_own) = scratch[len(groups) - 1:]
    rows = u_ref.shape[1]
    slot_rows = domains * each
    neighbours = shared_ref.shape[1]
    me = lax.axis_index("dom")
    near = flips(me, neighbours)
    peers = [lax.rem(me + apart, domains) for apart in range(1, domains)]
    greet(peers)
    prepare_corners(conn_ref, corner, high_ref, low_ref, rows * L)
    split_matrix(stiff_ref, matrix_ref)
    shared = shared_index(shared_ref)
    mass = mass_ref[...]
    u = [u_ref[c] for c in range(3)]
    v = [v_ref[c] for c in range(3)]
    for cycle in range(CYCLES):
        for c in range(3):
            x_ref[c] = u[c]
            vn_ref[c] = v[c]
            field[c] = u[c] + DAMP_RATIO * v[c]
        internal = internal_forces(
            field, total, corner, high_ref, low_ref, material_ref, matrix_ref, pieces)
        for c in range(3):
            field[c] = internal[c]
        found = field_lookup(field, shared)
        for b in range(neighbours):
            for c in range(3):
                own[cycle, b, c : c + 1, :] = found[c][b : b + 1, :]
        if cycle == 0:
            greeted(peers)
        copies = [send(own.at[cycle, b], rec.at[cycle, b], near_send.at[cycle, b],
                       near_recv.at[cycle, b], peer) for b, peer in enumerate(near)]
        for copy in copies:
            copy.start()
        if cycle == 0:
            slots(owner_ref, master_ref, normal_ref, slot_ref, ready, each, planes)
        for copy in copies:
            copy.wait()
        if cycle == 0:
            early = [pltpu.make_async_copy(ready.at[me], early_ref.at[me], early_own)]
            early += [send(ready.at[peer], early_ref.at[me], early_send.at[i], early_recv.at[i],
                           peer) for i, peer in enumerate(peers)]
            for copy in early:
                copy.start()
        u, v, assembled = advance(
            [x_ref[c] for c in range(3)], [vn_ref[c] for c in range(3)],
            [field[c] for c in range(3)], by_part(rec.at[cycle]), shared,
            [ext_ref[c] for c in range(3)], mass, [accel_ref[c] for c in range(3)],
            rows, neighbours, planes)
    for c in range(3):
        x_ref[c] = rest_ref[c] + u[c]
        vn_ref[c] = v[c]
        vals[4 + c] = ext_ref[c] - assembled[c] - mass * accel_ref[c]
    for copy in early:
        copy.wait()
    acc = None
    for t in range(0, slave_ref.shape[0], 8):
        sl = slice(t, t + 8)
        found = lookup(state_rows(x_ref, vn_ref, rows), slave_ref[sl, :])
        normal = [normal_ref[c, sl, :] for c in range(3)]
        along = sum(found[c] * normal[c] for c in range(3))
        speed = sum(found[3 + c] * normal[c] for c in range(3))
        slave_side[0, sl, :] = along
        slave_side[1, sl, :] = speed
        got = scatter_tile(slot_ref[sl, :], [along, speed], slot_rows, planes, t // 8 % 4)
        acc = got if acc is None else acc + got
    for c, value in enumerate(unstack(acc, 2, slot_rows, 2)):
        put_slots(pay, c, value, each)
    for t in range(slot_rows // 8):
        sl = slice(t * 8, t * 8 + 8)
        coded = slot_tile(early_ref, 3, t, each)
        master = jnp.maximum(coded - 0.5, 0.0).astype(jnp.int32)
        normal = [slot_tile(early_ref, c, t, each) for c in range(3)]
        found = lookup(state_rows(x_ref, vn_ref, rows), master)
        along = sum(found[c] * normal[c] for c in range(3))
        speed = sum(found[3 + c] * normal[c] for c in range(3))
        master_side[0, sl, :] = along
        master_side[1, sl, :] = speed
        step = 8 // each
        for j in range(step):
            pay[t * step + j, 2 * each : 3 * each, :] = along[j * each : (j + 1) * each]
            pay[t * step + j, 3 * each : 4 * each, :] = speed[j * each : (j + 1) * each]
    copies = [pltpu.make_async_copy(pay.at[me], back.at[me], own_sem)]
    copies += [send(pay.at[peer], back.at[me], pay_send.at[i], pay_recv.at[i], peer)
               for i, peer in enumerate(peers)]
    for copy in copies:
        copy.start()
    vals[0] = mass
    for c in range(3):
        vals[1 + c] = mass * x_ref[c]
    part_rows = sums.shape[1]
    part_sums(part_ref, vals, range(4), sums, planes)
    for copy in copies:
        copy.wait()
    total[...] = jnp.zeros_like(total)
    for t in range(slot_rows // 8):
        sl = slice(t * 8, t * 8 + 8)
        for c in range(2):
            table[c, sl, :] = slot_tile(back, 2 + c, t, each)
        coded = slot_tile(early_ref, 3, t, each)
        master = jnp.maximum(coded - 0.5, 0.0).astype(jnp.int32)
        normal = [slot_tile(early_ref, c, t, each) for c in range(3)]
        push = pushed(slot_tile(back, 0, t, each) - master_side[0, sl, :],
                      slot_tile(back, 1, t, each) - master_side[1, sl, :])
        push = jnp.where(coded > 0.5, push, 0.0)
        total[...] += scatter_tile(
            master, [-push * normal[c] for c in range(3)], rows, planes, t % 4)
    acc = None
    for t in range(0, slave_ref.shape[0], 8):
        sl = slice(t, t + 8)
        found = lookup(
            table_rows([lambda r, c=c: table[c, r : r + 1, :] for c in range(2)], slot_rows),
            slot_ref[sl, :])
        push = pushed(slave_side[0, sl, :] - found[0], slave_side[1, sl, :] - found[1])
        got = scatter_tile(slave_ref[sl, :], [push * normal_ref[c, sl, :] for c in range(3)],
                           rows, planes, t // 8 % 4)
        acc = got if acc is None else acc + got
    contact = unstack(total[...] + acc, 3, rows, 2)
    x = [x_ref[c] for c in range(3)]
    net = []
    for c in range(3):
        nv_ref[c] = vn_ref[c] + TIME_STEP * contact[c] / mass
        net.append(vals[4 + c] + contact[c])
        vals[4 + c] = net[c]
    vals[7] = x[1] * net[2] - x[2] * net[1]
    vals[8] = x[2] * net[0] - x[0] * net[2]
    vals[9] = x[0] * net[1] - x[1] * net[0]
    part_sums(part_ref, vals, range(4, 10), sums, planes)
    place = 0
    for g, (low, width) in enumerate(groups):
        size = 2**width
        digit = (me // 2**low) % size
        base = me - digit * 2**low
        copies = [pltpu.make_async_copy(sums, held[g].at[digit], sum_own.at[g])]
        for o in range(1, size):
            peer = base + ((digit + o) % size) * 2**low
            copies.append(send(sums, held[g].at[digit], sum_send.at[place],
                               sum_recv.at[place], peer))
            place += 1
        for copy in copies:
            copy.start()
        for copy in copies:
            copy.wait()
        value = held[g][0]
        for k in range(1, size):
            value = value + held[g][k]
        sums[...] = value
    for r in range(part_rows):
        wide = min(L, PARTS_SIZE - r * L)
        at = slice(r * L, r * L + wide)
        got = [sums[k, r : r + 1, 0:wide] for k in range(10)]
        own_mass = pmass_ref[0:1, at]
        mass_total = own_mass + got[0]
        centre = [(own_mass * pcentre_ref[c : c + 1, at] + got[1 + c]) / mass_total
                  for c in range(3)]
        force = got[4:7]
        swept = [centre[1] * force[2] - centre[2] * force[1],
                 centre[2] * force[0] - centre[0] * force[2],
                 centre[0] * force[1] - centre[1] * force[0]]
        for c in range(3):
            motion_ref[c : c + 1, at] = force[c] / mass_total
            motion_ref[3 + c : 4 + c, at] = (got[7 + c] - swept[c]) / pinertia_ref[c : c + 1, at]


VMEM = pl.BlockSpec(memory_space=pltpu.VMEM)
SMEM = pl.BlockSpec(memory_space=pltpu.SMEM)


def call(body, outs, scratch, specs, name, collective=None):
    return pl.pallas_call(
        body,
        out_shape=outs,
        in_specs=specs,
        out_specs=[VMEM] * len(outs),
        scratch_shapes=scratch,
        name=name,
        compiler_params=pltpu.CompilerParams(
            vmem_limit_bytes=48 * 2**20, collective_id=collective,
            has_side_effects=collective is not None),
    )


def f32(*shape):
    return jax.ShapeDtypeStruct(shape, F32)


def per_device(rest_pos, displacement, velocity, ext_force, node_mass, body_accel, connectivity,
               elem_material, stiffness, shared_nodes, contact_slave, contact_owner,
               contact_master, contact_normal, part_of_node, part_mass, part_center,
               part_inertia):
    domains = lax.axis_size("dom")
    neighbours = shared_nodes.shape[1]
    nodes = displacement.shape[1]
    rows = nodes // L
    contacts = contact_slave.shape[0]
    tiles = contacts // L
    each = -(-(4 * contacts // domains) // L)
    slot_rows = domains * each
    part_rows = -(-PARTS_SIZE // L)
    dma = pltpu.SemaphoreType.DMA

    u = displacement.reshape(3, rows, L)
    v = velocity.reshape(3, rows, L)
    ext = ext_force.reshape(3, rows, L)
    rest = rest_pos.reshape(3, rows, L)
    mass = node_mass.reshape(rows, L)
    owner = contact_owner.reshape(tiles, L)
    master = contact_master.reshape(tiles, L)
    slave = contact_slave.reshape(tiles, L)
    normal = contact_normal.reshape(3, tiles, L)


    materials, side = stiffness.shape[:2]
    groups = bit_groups(domains)
    count = sum(2**width - 1 for _, width in groups)
    sum_shape = (10, part_rows, L)
    blocks = connectivity.shape[1] // L
    node = pltpu.VMEM((3, rows, L), F32)
    near = pltpu.VMEM((CYCLES, neighbours, 8, L), F32)
    payload = pltpu.VMEM((domains, 4 * each, L), F32)
    far = [dma((domains - 1,))] * 2 + [dma]
    nodal_velocity, part_motion = call(
        functools.partial(window_body, each), [f32(3, rows, L), f32(6, PARTS_SIZE)],
        [node, pltpu.VMEM((6 * rows, L), F32), pltpu.VMEM(connectivity.shape, jnp.int32),
         pltpu.VMEM((blocks * 8, L), F32), pltpu.VMEM((blocks * 8, L), F32),
         pltpu.VMEM((2, 2, 24 * GROUP, L), F32), pltpu.VMEM((materials, side, 80), BF16),
         pltpu.VMEM((4, 22, 8, L), F32), near, near, node, node,
         pltpu.VMEM((tiles, L), jnp.int32), payload, payload, payload, payload,
         pltpu.VMEM((2, tiles, L), F32), pltpu.VMEM((2, slot_rows, L), F32),
         pltpu.VMEM((2, slot_rows, L), F32), pltpu.VMEM((10, rows, L), F32),
         pltpu.VMEM(sum_shape, F32)]
        + [pltpu.VMEM((2**width,) + sum_shape, F32) for _, width in groups]
        + [dma((CYCLES, neighbours))] * 2 + far + far
        + [dma((count,))] * 2 + [dma((len(groups),))],
        [VMEM] * 5 + [SMEM, VMEM, SMEM] + [VMEM] * 10, "window", 0)(
            u, v, rest, ext, mass, body_accel, connectivity, elem_material, stiffness,
            shared_nodes, slave, owner, master, normal, part_of_node.reshape(rows, L),
            part_mass.reshape(1, PARTS_SIZE), part_center, part_inertia)
    return nodal_velocity.reshape(3, nodes), part_motion


def solution(mesh):
    placed = (
        P(None, "dom"), P(None, "dom"), P(None, "dom"), P(None, "dom"), P("dom"), P(),
        P(None, "dom"), P("dom"), P(), P("dom", None, None), P("dom"), P("dom", None), P("dom"),
        P(None, "dom"), P("dom"), P(), P(), P(),
    )
    return jax.shard_map(
        per_device, mesh=mesh, in_specs=placed, out_specs=(P(None, "dom"), P()), check_vma=False
    )
```

time: 79.1 us -> 61.4 us (0.78)
  Pallas kernels: 72.1 us -> 55.7 us
  local copies, waits for them, and re-layouts: 5.88 us -> 4.57 us
    pallas_call x4 -> x1, Pallas kernels: 72.1 us -> 55.7 us  [per_device(): call(functools.partial(window_body, each), [f32(3, rows, L), f32(6, PARTS...]
    unnamed x34, local copies, waits for them, and re-layouts: 4.97 us -> 3.63 us
where the time goes in v2:
time: 61.4 us; the launch traced here: 61.1 us
  Pallas kernels  55.7 us (91%)
  local copies, waits for them, and re-layouts  4.57 us (7%)
  between operations  0.82 us (1%)
    pallas_call x1, Pallas kernels, per_device(): call(functools.partial(window_body, each), [f32(3, rows, L), f32(6, PARTS...  55.7 us
    unnamed x34, local copies, waits for them, and re-layouts  3.63 us

profile of v2, /device:TPU:0, one launch (start us, length us, event | category | flops | bytes accessed | tf_op | source)
XLA Modules:
  0.0 61.1 jit_solution(2821746027960119529)
XLA Ops:
  0.6 0.0 copy-start.12
  0.6 0.7 %copy.20.shared_ref = s32[1,5,128]{2,1,0:T(8,128)S(1)} copy(s32[1,5,128]{2,0,1:T(1,128)} %param.27) | data formatting | bytes 5120 | tf_op args[9]
  1.4 0.8 %copy.34 = f32[1,3,16,128]{3,2,1,0:T(8,128)S(1)} copy(f32[1,3,16,128]{3,1,2,0:T(4,128)} %bitcast.39) | data formatting | bytes 49152
  2.1 0.0 copy-done.12
  2.1 0.0 copy-start.13
  2.1 0.0 copy-start.14
  2.1 0.0 copy-start.2
  2.1 0.0 copy-start.3
  2.1 0.0 copy-start.4
  2.2 0.0 copy-start.5
  2.2 0.0 copy-start.6
  2.2 0.0 copy-start.7
  2.2 0.0 copy-start.8
  2.2 0.9 %copy_bitcast_fusion.1 = (f32[3,32,128]{2,1,0:T(8,128)S(1)}, f32[3,32,128]{2,1,0:T(8,128)S(1)}) fusion(f32[1,3,32,128]{3,1,2,0:T(4,128)S(1)} %bitcast.34, f32[1,3,32,128]{3,1,2,0:T(4,128)} %bitcast.35), kind=kLoop, calls=%fused_computation.1 | loop fusion | bytes 196608 | tf_op jit(solution)/shard_map/reshape | solution.py:495
  3.1 0.0 copy-start
  3.1 0.0 copy-done.13
  3.2 0.0 copy-done.14
  3.2 0.0 copy-start.1
  3.2 0.0 copy-start.9
  3.2 0.0 copy-start.10
  3.2 0.0 copy-start.11
  3.2 0.0 copy-done.2
  3.2 0.0 copy-done.3
  3.2 0.0 copy-done.4
  3.3 0.0 copy-done.5
  3.3 0.0 copy-done.6
  3.3 0.0 copy-done.7
  3.3 0.0 copy-done.8
  3.3 0.7 %copy-done = s32[8,4096]{1,0:T(8,128)S(1)} copy-done((s32[8,4096]{1,0:T(8,128)S(1)}, s32[8,4096]{1,0:T(8,128)}, u32[]{:S(2)}) %copy-start) | copy-done | bytes 131096
  4.0 0.1 copy-done.1
  4.1 0.0 copy-done.9
  4.1 0.0 copy-done.10
  4.1 0.0 copy-done.11
  4.1 55.7 %window.1 = (f32[3,32,128]{2,1,0:T(8,128)S(1)}, f32[6,400]{1,0:T(8,128)S(1)}) custom-call(f32[3,32,128]{2,1,0:T(8,128)S(1)} %get-tuple-element.9.u_ref, f32[3,32,128]{2,1,0:T(8,128)S(1)} %get-tuple-element.8.v_ref, f32[3,32,128]{2,1,0:T(8,128)S(1)} %get-tuple-element.7.rest_ref, f32[3,32,128]{2,1,0:T(8,128)S(1)} %get-tuple-element.6.ext_ref, ...), custom_call_target="tpu_custom_call" | custom-call | tf_op jit(solution)/shard_map/window/pallas_call | solution.py:513
  59.8 0.7 %copy.33 = f32[1,3,32,128]{3,1,2,0:T(4,128)} copy(f32[1,3,32,128]{3,2,1,0:T(8,128)S(1)} %bitcast.27) | data formatting | bytes 98304
  60.5 0.6 copy.36
  (1 shorter events, 0.0 us)
Async XLA Ops:
  0.6 1.5 %copy-start.12 = (f32[3,4096]{1,0:T(4,128)S(1)}, f32[3,4096]{1,0:T(4,128)}, u32[]{:S(2)}) copy-start(f32[3,4096]{1,0:T(4,128)} %param.21) | copy-start | bytes 147460
  2.1 1.0 %copy-start.13 = (f32[3,4096]{1,0:T(4,128)S(1)}, f32[3,4096]{1,0:T(4,128)}, u32[]{:S(2)}) copy-start(f32[3,4096]{1,0:T(4,128)} %param.20) | copy-start | bytes 147460
  2.1 1.0 %copy-start.14 = (f32[3,4096]{1,0:T(4,128)S(1)}, f32[3,4096]{1,0:T(4,128)}, u32[]{:S(2)}) copy-start(f32[3,4096]{1,0:T(4,128)} %param.19) | copy-start | bytes 147460
  2.1 1.1 %copy-start.2 = (f32[4096]{0:T(1024)S(1)}, f32[4096]{0:T(1024)}, u32[]{:S(2)}) copy-start(f32[4096]{0:T(1024)} %param.22) | copy-start | bytes 49156
  2.1 1.1 %copy-start.3 = (s32[4096]{0:T(1024)S(1)}, s32[4096]{0:T(1024)}, u32[]{:S(2)}) copy-start(s32[4096]{0:T(1024)} %param.32) | copy-start | bytes 49156
  2.1 1.1 %copy-start.4 = (s32[2048]{0:T(1024)S(1)}, s32[2048]{0:T(1024)}, u32[]{:S(2)}) copy-start(s32[2048]{0:T(1024)} %param.28) | copy-start | bytes 24580
  2.2 1.1 %copy-start.5 = (s32[2048,1]{0,1:T(1,128)S(1)}, s32[2048,1]{0,1:T(1,128)}, u32[]{:S(2)}) copy-start(s32[2048,1]{0,1:T(1,128)} %param.29) | copy-start | bytes 24580
  2.2 1.1 %copy-start.6 = (s32[2048]{0:T(1024)S(1)}, s32[2048]{0:T(1024)}, u32[]{:S(2)}) copy-start(s32[2048]{0:T(1024)} %param.30) | copy-start | bytes 24580
  2.2 1.1 %copy-start.7 = (f32[3,400]{1,0:T(4,128)S(1)}, f32[3,400]{1,0:T(4,128)}, u32[]{:S(2)}) copy-start(f32[3,400]{1,0:T(4,128)} %pcentre_ref.1) | copy-start | bytes 14404
  2.2 1.1 %copy-start.8 = (f32[3,400]{1,0:T(4,128)S(1)}, f32[3,400]{1,0:T(4,128)}, u32[]{:S(2)}) copy-start(f32[3,400]{1,0:T(4,128)} %pinertia_ref.1) | copy-start | bytes 14404
  3.1 0.9 %copy-start = (s32[8,4096]{1,0:T(8,128)S(1)}, s32[8,4096]{1,0:T(8,128)}, u32[]{:S(2)}) copy-start(s32[8,4096]{1,0:T(8,128)} %conn_ref.1) | copy-start | bytes 393220
  3.2 0.9 %copy-start.1 = (f32[8,24,24]{2,1,0:T(8,128)S(1)}, f32[8,24,24]{2,1,0:T(8,128)}, u32[]{:S(2)}) copy-start(f32[8,24,24]{2,1,0:T(8,128)} %stiff_ref.1) | copy-start | bytes 55300
  3.2 0.9 %copy-start.9 = (f32[400]{0:T(512)S(1)}, f32[400]{0:T(512)}, u32[]{:S(2)}) copy-start(f32[400]{0:T(512)} %param.33) | copy-start | bytes 4804
  3.2 0.9 %copy-start.10 = (f32[3]{0:T(128)S(1)}, f32[3]{0:T(128)}, u32[]{:S(2)}) copy-start(f32[3]{0:T(128)} %accel_ref.1) | copy-start | bytes 40
  3.2 0.9 %copy-start.11 = (s32[32]{0:T(128)S(1)}, s32[32]{0:T(128)}, u32[]{:S(2)}) copy-start(s32[32]{0:T(128)} %material_ref.1) | copy-start | bytes 388
